TPU v7x, 32 devices: a whole 2x2x4 slice. The times are simulated.
32 devices in a mesh: groups: 2 (over y), seq: 4 (over z), tensor: 2 (over x), sub: 2 (over core).
Axes of the slice: x: 2, y: 2, z: 4, core: 2. Of those that a mesh axis runs over, the one named last changes fastest.
Arguments:
- features: bfloat16 [3072, 3, 8192], P(('groups', 'seq'), None, ('tensor', 'sub')), parts along dimension 0, may hold values from -6 to 6
- short_filter: float32 [7, 8192], P(None, ('tensor', 'sub')), may hold values from -5 to 5
- medium_filter: float32 [128, 8192], P(None, ('tensor', 'sub')), may hold values from -1.25 to 1.25
- skip_gain: float32 [8192], P(('tensor', 'sub')), may hold values from 0.5 to 1.5
- attn_query: bfloat16 [3072, 8192], P(('groups', 'seq'), ('tensor', 'sub')), parts along dimension 0, may hold values from -100 to 100
- attn_key: bfloat16 [3072, 8192], P(('groups', 'seq'), ('tensor', 'sub')), parts along dimension 0, may hold values from -5 to 5
- attn_value: bfloat16 [3072, 8192], P(('groups', 'seq'), ('tensor', 'sub')), parts along dimension 0, may hold values from -6 to 6
- lengths: int32 [8], P('groups'), parts along dimension 0, may hold values from 1 to 768, 1536 in all
Outputs:
- hyena_out: bfloat16 [3072, 8192], P(('groups', 'seq'), ('tensor', 'sub')), parts along dimension 0
- attn_out: bfloat16 [3072, 8192], P(('groups', 'seq'), ('tensor', 'sub')), parts along dimension 0
There are 2 independent parts, one for each index of `groups`. A program takes and returns all parts, laid end to end along the dimension named above; an argument that names none is the same for every part. Nothing has to cross between parts.
Inputs may be any that keep to these rules, and one draw needn't show every extreme that they name: 4 documents packed end to end in order; their lengths sum to 1536 and the longest is exactly 768 tokens.
All inputs are finite; a program needn't handle non-finite values.
Results may differ from a plain program's by a relative error of at most 0.0051.
Values may be sent and summed in bfloat16 or wider, within the bound.
A program may use at most 192 MiB of HBM per device.

v0:
```python
import math

import jax
import jax.numpy as jnp
from jax import lax
from jax.sharding import PartitionSpec as P

HD = 128


def passed_along(value, axis, by):
    length = lax.axis_size(axis)
    pairs = [(i, i + by) for i in range(length) if 0 <= i + by < length]
    return lax.ppermute(value, axis, pairs)


def doc_of(positions, lengths):
    doc_ends = jnp.cumsum(lengths, dtype=jnp.int32)
    return jnp.sum(
        (positions[:, None] >= doc_ends[None, :]).astype(jnp.int32), axis=1, dtype=jnp.int32
    )


def hyena_mix(features, short_filter, medium_filter, skip_gain, lengths):
    row_count = features.shape[0]
    medium_taps = medium_filter.shape[0]
    rim_rows = medium_taps - 1
    span_index = lax.axis_index("seq")
    queries = features[:, 0].astype(jnp.float32)
    gated = (features[:, 1].astype(jnp.float32) * features[:, 2].astype(jnp.float32)).astype(
        jnp.bfloat16
    )
    gated = lax.optimization_barrier(gated)
    carried = passed_along(gated[row_count - rim_rows :], "seq", 1)
    extended = jnp.concatenate((carried, gated), axis=0)
    ext_positions = (
        span_index * row_count - rim_rows + jnp.arange(row_count + rim_rows, dtype=jnp.int32)
    )
    ext_docs = doc_of(ext_positions, lengths)
    ext_live = ext_positions >= 0
    own_docs = ext_docs[rim_rows:]

    def tap_term(tap_index, filter_bank):
        first_row = rim_rows - tap_index
        window = lax.dynamic_slice_in_dim(extended, first_row, row_count, 0).astype(jnp.float32)
        same_doc = lax.dynamic_slice_in_dim(ext_docs, first_row, row_count, 0) == own_docs
        live_mask = lax.dynamic_slice_in_dim(ext_live, first_row, row_count, 0)
        keep_mask = (same_doc & live_mask).astype(jnp.float32)[:, None]
        taps = lax.dynamic_index_in_dim(filter_bank, tap_index, 0, keepdims=False)
        return taps[None, :] * window * keep_mask

    short_sum = jnp.zeros(gated.shape, jnp.float32)
    for tap_index in range(short_filter.shape[0]):
        short_sum = short_sum + tap_term(tap_index, short_filter)

    def tap_block(block_index, partial_value):
        for offset in range(8):
            partial_value = partial_value + tap_term(block_index * 8 + offset, medium_filter)
        return partial_value

    medium_sum = lax.fori_loop(0, medium_taps // 8, tap_block, jnp.zeros(gated.shape, jnp.float32))
    mixed = queries * (short_sum + medium_sum + skip_gain[None, :] * gated.astype(jnp.float32))
    return mixed.astype(jnp.bfloat16)


def attention_mix(attn_query, attn_key, attn_value, lengths):
    row_count, col_count = attn_query.shape
    heads_here = col_count // HD
    span_index = lax.axis_index("seq")
    query_positions = span_index * row_count + jnp.arange(row_count, dtype=jnp.int32)
    query_docs = doc_of(query_positions, lengths)
    query_heads = attn_query.reshape(row_count, heads_here, HD)
    score_scale = HD ** (-0.5)
    last_query = query_positions[row_count - 1]
    first_query_doc = query_docs[0]

    def absorb(state_now, key_block, value_block, first_row):
        key_count = key_block.shape[0]
        last_key = first_row + key_count - 1
        last_key_doc = doc_of(jnp.reshape(last_key, (1,)), lengths)[0]
        masked_out = (first_row > last_query) | (last_key < 0) | (last_key_doc < first_query_doc)

        def compute(state_in):
            running_max, running_total, running_sum = state_in
            key_heads = key_block.reshape(key_count, heads_here, HD)
            value_heads = value_block.reshape(key_count, heads_here, HD)
            scores = (
                jnp.einsum(
                    "rhd,nhd->hrn", query_heads, key_heads, preferred_element_type=jnp.float32
                )
                * score_scale
            )
            key_positions = first_row + jnp.arange(key_count, dtype=jnp.int32)
            key_docs = doc_of(key_positions, lengths)
            allowed = (
                (key_positions[None, :] <= query_positions[:, None])
                & (key_docs[None, :] == query_docs[:, None])
                & (key_positions >= 0)[None, :]
            )
            masked = jnp.where(allowed[None], scores, -1e30)
            new_max = jnp.maximum(running_max, jnp.max(masked, axis=2))
            rescale = jnp.exp(running_max - new_max)
            weights = jnp.where(allowed[None], jnp.exp(scores - new_max[:, :, None]), 0.0)
            new_total = running_total * rescale + jnp.sum(weights, axis=2)
            product = jnp.einsum(
                "hrn,nhd->hrd",
                weights.astype(jnp.bfloat16),
                value_heads,
                preferred_element_type=jnp.float32,
            )
            new_sum = running_sum * rescale[:, :, None] + product
            return (new_max, new_total, new_sum)

        def keep_state(state_in):
            return state_in

        return lax.cond(masked_out, keep_state, compute, state_now)

    def fold_keys(state_now, pieces, first_row):
        key_all, value_all = pieces
        key_count = key_all.shape[0]
        block_rows = math.gcd(key_count, 1536)
        if block_rows == key_count:
            return absorb(state_now, key_all, value_all, first_row)
        block_total = key_count // block_rows
        key_blocks = key_all.reshape(block_total, block_rows, col_count)
        value_blocks = value_all.reshape(block_total, block_rows, col_count)

        def scan_step(state_inner, block_items):
            key_block, value_block, block_index = block_items
            return (
                absorb(state_inner, key_block, value_block, first_row + block_index * block_rows),
                None,
            )

        state_now, unused = lax.scan(
            scan_step,
            state_now,
            (key_blocks, value_blocks, jnp.arange(block_total, dtype=jnp.int32)),
        )
        return state_now

    initial = (
        jnp.full((heads_here, row_count), -1e30, jnp.float32),
        jnp.zeros((heads_here, row_count), jnp.float32),
        jnp.zeros((heads_here, row_count, HD), jnp.float32),
    )
    state_now = fold_keys(
        initial,
        (
            lax.all_gather(attn_key, "seq", axis=0, tiled=True),
            lax.all_gather(attn_value, "seq", axis=0, tiled=True),
        ),
        jnp.int32(0),
    )
    running_max, running_total, running_sum = state_now
    result = running_sum / running_total[:, :, None]
    return result.transpose(1, 0, 2).reshape(row_count, col_count).astype(jnp.bfloat16)


def local(
    features, short_filter, medium_filter, skip_gain, attn_query, attn_key, attn_value, lengths
):
    hyena_out = hyena_mix(features, short_filter, medium_filter, skip_gain, lengths)
    attn_out = attention_mix(attn_query, attn_key, attn_value, lengths)
    return (hyena_out, attn_out)


def solution(mesh):
    in_specs = (
        P(("groups", "seq"), None, ("tensor", "sub")),
        P(None, ("tensor", "sub")),
        P(None, ("tensor", "sub")),
        P(("tensor", "sub")),
        P(("groups", "seq"), ("tensor", "sub")),
        P(("groups", "seq"), ("tensor", "sub")),
        P(("groups", "seq"), ("tensor", "sub")),
        P("groups"),
    )
    out_specs = (P(("groups", "seq"), ("tensor", "sub")), P(("groups", "seq"), ("tensor", "sub")))
    return jax.shard_map(local, mesh=mesh, in_specs=in_specs, out_specs=out_specs, check_vma=False)
```

profile of v0, /device:TPU:10, one launch (start us, length us, event | category | flops | bytes accessed | tf_op | source)
XLA Modules:
  0.0 306.4 jit_solution(14949909395084193033)
XLA Ops:
  18.7 20.4 %collective-permute-done = bf16[127,2048]{1,0:T(8,128)(2,1)S(1)} collective-permute-done((bf16[127,2048]{1,0:T(8,128)(2,1)S(1)}, bf16[127,2048]{1,0:T(8,128)(2,1)S(1)}, u32[]{:S(2)}, u32[]{:S(2)}) %collective-permute-start) | collective-permute-done | bytes 520224 | tf_op jit(solution)/shard_map/ppermute | solution.py:14
  41.1 180.1 %while.17 = (s32[]{:T(128)}, f32[384,2048]{1,0:T(8,128)}, f32[128,2048]{1,0:T(8,128)}, bf16[511,2048]{1,0:T(8,128)(2,1)S(1)}, s32[511]{0:T(512)S(1)}, /*index=5*...) while((s32[]{:T(128)}, f32[384,2048]{1,0:T(8,128)}, ...), condition=%wide.region_3.4_spmd.clone, body=%wide.region_2.3_spmd.clone.sunk | while | flops 25961540 | bytes 19113524 | solution.py:61
  42.6 8.7 %fusion.84 = f32[384,2048]{1,0:T(8,128)} fusion(f32[384,2048]{1,0:T(8,128)} %get-tuple-element.425, f32[384]{0:T(512)S(1)} %get-tuple-element.382, bf16[511,2048]{1,0:T(8,128)(2,1)S(1)} %get-tuple-element.453, s32[]{:T(128)S(6)} %select_n.250, f32[2048]{0:T(1024)S(1)} %bitcast.76, f32[384]{0:T(512)S(1)} %get-tuple-element.384, s32[]{:T(128)S(6)} %select_n.251, ...), kind=kLoop, calls=%fused_computation.30.clone.1 | loop fusion | flops 25952256 | bytes 18952224 | tf_op jit(solution)/shard_map/while/body/eval_jaxpr/add | solution.py:58
  52.7 9.9 %fusion.84 = f32[384,2048]{1,0:T(8,128)} fusion(f32[384,2048]{1,0:T(8,128)} %get-tuple-element.425, f32[384]{0:T(512)S(1)} %get-tuple-element.382, bf16[511,2048]{1,0:T(8,128)(2,1)S(1)} %get-tuple-element.453, s32[]{:T(128)S(6)} %select_n.250, f32[2048]{0:T(1024)S(1)} %bitcast.76, f32[384]{0:T(512)S(1)} %get-tuple-element.384, s32[]{:T(128)S(6)} %select_n.251, ...), kind=kLoop, calls=%fused_computation.30.clone.1 | loop fusion | flops 25952256 | bytes 18952224 | tf_op jit(solution)/shard_map/while/body/eval_jaxpr/add | solution.py:58
  64.0 9.9 %fusion.84 = f32[384,2048]{1,0:T(8,128)} fusion(f32[384,2048]{1,0:T(8,128)} %get-tuple-element.425, f32[384]{0:T(512)S(1)} %get-tuple-element.382, bf16[511,2048]{1,0:T(8,128)(2,1)S(1)} %get-tuple-element.453, s32[]{:T(128)S(6)} %select_n.250, f32[2048]{0:T(1024)S(1)} %bitcast.76, f32[384]{0:T(512)S(1)} %get-tuple-element.384, s32[]{:T(128)S(6)} %select_n.251, ...), kind=kLoop, calls=%fused_computation.30.clone.1 | loop fusion | flops 25952256 | bytes 18952224 | tf_op jit(solution)/shard_map/while/body/eval_jaxpr/add | solution.py:58
  75.3 9.9 %fusion.84 = f32[384,2048]{1,0:T(8,128)} fusion(f32[384,2048]{1,0:T(8,128)} %get-tuple-element.425, f32[384]{0:T(512)S(1)} %get-tuple-element.382, bf16[511,2048]{1,0:T(8,128)(2,1)S(1)} %get-tuple-element.453, s32[]{:T(128)S(6)} %select_n.250, f32[2048]{0:T(1024)S(1)} %bitcast.76, f32[384]{0:T(512)S(1)} %get-tuple-element.384, s32[]{:T(128)S(6)} %select_n.251, ...), kind=kLoop, calls=%fused_computation.30.clone.1 | loop fusion | flops 25952256 | bytes 18952224 | tf_op jit(solution)/shard_map/while/body/eval_jaxpr/add | solution.py:58
  86.6 9.9 %fusion.84 = f32[384,2048]{1,0:T(8,128)} fusion(f32[384,2048]{1,0:T(8,128)} %get-tuple-element.425, f32[384]{0:T(512)S(1)} %get-tuple-element.382, bf16[511,2048]{1,0:T(8,128)(2,1)S(1)} %get-tuple-element.453, s32[]{:T(128)S(6)} %select_n.250, f32[2048]{0:T(1024)S(1)} %bitcast.76, f32[384]{0:T(512)S(1)} %get-tuple-element.384, s32[]{:T(128)S(6)} %select_n.251, ...), kind=kLoop, calls=%fused_computation.30.clone.1 | loop fusion | flops 25952256 | bytes 18952224 | tf_op jit(solution)/shard_map/while/body/eval_jaxpr/add | solution.py:58
  97.9 9.9 %fusion.84 = f32[384,2048]{1,0:T(8,128)} fusion(f32[384,2048]{1,0:T(8,128)} %get-tuple-element.425, f32[384]{0:T(512)S(1)} %get-tuple-element.382, bf16[511,2048]{1,0:T(8,128)(2,1)S(1)} %get-tuple-element.453, s32[]{:T(128)S(6)} %select_n.250, f32[2048]{0:T(1024)S(1)} %bitcast.76, f32[384]{0:T(512)S(1)} %get-tuple-element.384, s32[]{:T(128)S(6)} %select_n.251, ...), kind=kLoop, calls=%fused_computation.30.clone.1 | loop fusion | flops 25952256 | bytes 18952224 | tf_op jit(solution)/shard_map/while/body/eval_jaxpr/add | solution.py:58
  109.5 9.9 %fusion.84 = f32[384,2048]{1,0:T(8,128)} fusion(f32[384,2048]{1,0:T(8,128)} %get-tuple-element.425, f32[384]{0:T(512)S(1)} %get-tuple-element.382, bf16[511,2048]{1,0:T(8,128)(2,1)S(1)} %get-tuple-element.453, s32[]{:T(128)S(6)} %select_n.250, f32[2048]{0:T(1024)S(1)} %bitcast.76, f32[384]{0:T(512)S(1)} %get-tuple-element.384, s32[]{:T(128)S(6)} %select_n.251, ...), kind=kLoop, calls=%fused_computation.30.clone.1 | loop fusion | flops 25952256 | bytes 18952224 | tf_op jit(solution)/shard_map/while/body/eval_jaxpr/add | solution.py:58
  120.8 9.9 %fusion.84 = f32[384,2048]{1,0:T(8,128)} fusion(f32[384,2048]{1,0:T(8,128)} %get-tuple-element.425, f32[384]{0:T(512)S(1)} %get-tuple-element.382, bf16[511,2048]{1,0:T(8,128)(2,1)S(1)} %get-tuple-element.453, s32[]{:T(128)S(6)} %select_n.250, f32[2048]{0:T(1024)S(1)} %bitcast.76, f32[384]{0:T(512)S(1)} %get-tuple-element.384, s32[]{:T(128)S(6)} %select_n.251, ...), kind=kLoop, calls=%fused_computation.30.clone.1 | loop fusion | flops 25952256 | bytes 18952224 | tf_op jit(solution)/shard_map/while/body/eval_jaxpr/add | solution.py:58
  132.1 9.9 %fusion.84 = f32[384,2048]{1,0:T(8,128)} fusion(f32[384,2048]{1,0:T(8,128)} %get-tuple-element.425, f32[384]{0:T(512)S(1)} %get-tuple-element.382, bf16[511,2048]{1,0:T(8,128)(2,1)S(1)} %get-tuple-element.453, s32[]{:T(128)S(6)} %select_n.250, f32[2048]{0:T(1024)S(1)} %bitcast.76, f32[384]{0:T(512)S(1)} %get-tuple-element.384, s32[]{:T(128)S(6)} %select_n.251, ...), kind=kLoop, calls=%fused_computation.30.clone.1 | loop fusion | flops 25952256 | bytes 18952224 | tf_op jit(solution)/shard_map/while/body/eval_jaxpr/add | solution.py:58
  143.4 9.9 %fusion.84 = f32[384,2048]{1,0:T(8,128)} fusion(f32[384,2048]{1,0:T(8,128)} %get-tuple-element.425, f32[384]{0:T(512)S(1)} %get-tuple-element.382, bf16[511,2048]{1,0:T(8,128)(2,1)S(1)} %get-tuple-element.453, s32[]{:T(128)S(6)} %select_n.250, f32[2048]{0:T(1024)S(1)} %bitcast.76, f32[384]{0:T(512)S(1)} %get-tuple-element.384, s32[]{:T(128)S(6)} %select_n.251, ...), kind=kLoop, calls=%fused_computation.30.clone.1 | loop fusion | flops 25952256 | bytes 18952224 | tf_op jit(solution)/shard_map/while/body/eval_jaxpr/add | solution.py:58
  154.7 9.9 %fusion.84 = f32[384,2048]{1,0:T(8,128)} fusion(f32[384,2048]{1,0:T(8,128)} %get-tuple-element.425, f32[384]{0:T(512)S(1)} %get-tuple-element.382, bf16[511,2048]{1,0:T(8,128)(2,1)S(1)} %get-tuple-element.453, s32[]{:T(128)S(6)} %select_n.250, f32[2048]{0:T(1024)S(1)} %bitcast.76, f32[384]{0:T(512)S(1)} %get-tuple-element.384, s32[]{:T(128)S(6)} %select_n.251, ...), kind=kLoop, calls=%fused_computation.30.clone.1 | loop fusion | flops 25952256 | bytes 18952224 | tf_op jit(solution)/shard_map/while/body/eval_jaxpr/add | solution.py:58
  166.1 9.9 %fusion.84 = f32[384,2048]{1,0:T(8,128)} fusion(f32[384,2048]{1,0:T(8,128)} %get-tuple-element.425, f32[384]{0:T(512)S(1)} %get-tuple-element.382, bf16[511,2048]{1,0:T(8,128)(2,1)S(1)} %get-tuple-element.453, s32[]{:T(128)S(6)} %select_n.250, f32[2048]{0:T(1024)S(1)} %bitcast.76, f32[384]{0:T(512)S(1)} %get-tuple-element.384, s32[]{:T(128)S(6)} %select_n.251, ...), kind=kLoop, calls=%fused_computation.30.clone.1 | loop fusion | flops 25952256 | bytes 18952224 | tf_op jit(solution)/shard_map/while/body/eval_jaxpr/add | solution.py:58
  177.4 9.9 %fusion.84 = f32[384,2048]{1,0:T(8,128)} fusion(f32[384,2048]{1,0:T(8,128)} %get-tuple-element.425, f32[384]{0:T(512)S(1)} %get-tuple-element.382, bf16[511,2048]{1,0:T(8,128)(2,1)S(1)} %get-tuple-element.453, s32[]{:T(128)S(6)} %select_n.250, f32[2048]{0:T(1024)S(1)} %bitcast.76, f32[384]{0:T(512)S(1)} %get-tuple-element.384, s32[]{:T(128)S(6)} %select_n.251, ...), kind=kLoop, calls=%fused_computation.30.clone.1 | loop fusion | flops 25952256 | bytes 18952224 | tf_op jit(solution)/shard_map/while/body/eval_jaxpr/add | solution.py:58
  188.7 9.9 %fusion.84 = f32[384,2048]{1,0:T(8,128)} fusion(f32[384,2048]{1,0:T(8,128)} %get-tuple-element.425, f32[384]{0:T(512)S(1)} %get-tuple-element.382, bf16[511,2048]{1,0:T(8,128)(2,1)S(1)} %get-tuple-element.453, s32[]{:T(128)S(6)} %select_n.250, f32[2048]{0:T(1024)S(1)} %bitcast.76, f32[384]{0:T(512)S(1)} %get-tuple-element.384, s32[]{:T(128)S(6)} %select_n.251, ...), kind=kLoop, calls=%fused_computation.30.clone.1 | loop fusion | flops 25952256 | bytes 18952224 | tf_op jit(solution)/shard_map/while/body/eval_jaxpr/add | solution.py:58
  200.0 9.9 %fusion.84 = f32[384,2048]{1,0:T(8,128)} fusion(f32[384,2048]{1,0:T(8,128)} %get-tuple-element.425, f32[384]{0:T(512)S(1)} %get-tuple-element.382, bf16[511,2048]{1,0:T(8,128)(2,1)S(1)} %get-tuple-element.453, s32[]{:T(128)S(6)} %select_n.250, f32[2048]{0:T(1024)S(1)} %bitcast.76, f32[384]{0:T(512)S(1)} %get-tuple-element.384, s32[]{:T(128)S(6)} %select_n.251, ...), kind=kLoop, calls=%fused_computation.30.clone.1 | loop fusion | flops 25952256 | bytes 18952224 | tf_op jit(solution)/shard_map/while/body/eval_jaxpr/add | solution.py:58
  211.3 9.9 %fusion.84 = f32[384,2048]{1,0:T(8,128)} fusion(f32[384,2048]{1,0:T(8,128)} %get-tuple-element.425, f32[384]{0:T(512)S(1)} %get-tuple-element.382, bf16[511,2048]{1,0:T(8,128)(2,1)S(1)} %get-tuple-element.453, s32[]{:T(128)S(6)} %select_n.250, f32[2048]{0:T(1024)S(1)} %bitcast.76, f32[384]{0:T(512)S(1)} %get-tuple-element.384, s32[]{:T(128)S(6)} %select_n.251, ...), kind=kLoop, calls=%fused_computation.30.clone.1 | loop fusion | flops 25952256 | bytes 18952224 | tf_op jit(solution)/shard_map/while/body/eval_jaxpr/add | solution.py:58
  221.2 13.1 %fusion.54 = bf16[384,2048]{1,0:T(8,128)(2,1)} fusion(f32[384,2048]{1,0:T(8,128)} %get-tuple-element.246, bf16[384,2048]{1,0:T(8,128)(2,1)} %copy-done, bf16[127,2048]{1,0:T(8,128)(2,1)S(1)} %collective-permute-done, f32[2048]{0:T(1024)S(1)} %copy-done.2, f32[384]{0:T(512)S(1)} %get-tuple-element.317, f32[2048]{0:T(1024)S(1)} %bitcast.88, ...), kind=kLoop, calls=%fused_computation.82 | loop fusion | flops 40108032 | bytes 8460800 | tf_op jit(solution)/shard_map/convert_element_type | solution.py:63
  234.3 9.0 %all-gather.5.cloned.1.call-done = bf16[1536,2048]{1,0:T(8,128)(2,1)} async-done(((bf16[384,2048]{1,0:T(8,128)(2,1)}), bf16[1536,2048]{1,0:T(8,128)(2,1)}) %all-gather.5.cloned.1.call-update) | async-done | bytes 6291472 | tf_op jit(solution)/shard_map/all_gather | solution.py:152
  243.3 54.4 %conditional.1 = (f32[16,384]{1,0:T(8,128)S(1)}, f32[16,384,128]{2,1,0:T(8,128)S(1)}) conditional(s32[]{:T(128)} %convert_element_type.302, (s32[384]{0:T(512)S(1)}, s32[4]{0:T(128)S(1)}, s32[384]{0:T(512)S(1)}, bf16[384,2048]{1,0:T(8,128)(2,1)}, bf16[1536,2048]{1,0:T(8,128)(2,1)}, /*index=5*/bf16[1536,2048]{1,0:T(8,128)(2,1)}) %tuple.98, () %tuple.43), branch_computations={%region_6.11_spmd, %region_11.12_spmd} | conditional | flops 4938238464 | bytes 133192768 | solution.py:117
  244.2 18.3 %select_reduce_fusion = (f32[16,384]{1,0:T(8,128)S(1)}, f32[16,384,1536]{2,1,0:T(8,128)}) fusion(pred[384,1536]{1,0:T(8,128)(4,1)S(1)} %fusion.10, bf16[1536,2048]{1,0:T(8,128)(2,1)} %get-tuple-element.239, bf16[384,2048]{1,0:T(8,128)(2,1)} %get-tuple-element.250), kind=kOutput, calls=%fused_computation.1 | convolution fusion | flops 2444224512 | bytes 46227456 | tf_op jit(solution)/shard_map/cond/branch_0_fun/rhd,nhd->hrn/dot_general | solution.py:88
  262.4 17.6 %fusion.1 = f32[16,384]{1,0:T(8,128)S(1)} fusion(f32[16,384,1536]{2,1,0:T(8,128)} %get-tuple-element.292, f32[16,384]{1,0:T(8,128)S(1)} %broadcast_maximum_fusion, pred[384,1536]{1,0:T(8,128)(4,1)S(1)} %fusion.10), kind=kLoop, calls=%fused_computation.3 | loop fusion | flops 37742592 | bytes 38387712 | tf_op jit(solution)/shard_map/cond/branch_0_fun/reduce_sum | solution.py:104
  280.1 17.6 %fusion.11 = f32[16,384,128]{2,1,0:T(8,128)S(1)} fusion(f32[16,384,1536]{2,1,0:T(8,128)} %get-tuple-element.292, f32[16,384]{1,0:T(8,128)S(1)} %broadcast_maximum_fusion, pred[384,1536]{1,0:T(8,128)(4,1)S(1)} %fusion.10, f32[16,384]{1,0:T(8,128)S(1)} %get-tuple-element.289, bf16[1536,2048]{1,0:T(8,128)(2,1)} %get-tuple-element.240), kind=kOutput, calls=%fused_computation.13 | convolution fusion | flops 2454454272 | bytes 47824896 | tf_op jit(solution)/shard_map/cond/branch_0_fun/hrn,nhd->hrd/dot_general | solution.py:105
  (68 shorter events, 36.6 us)
Async XLA Ops:
  7.2 227.2 %all-gather.3.cloned.1.call-start = ((), (), s32[]{:S(2)}) async-start(), calls=%async_computation | async-start | bytes 7864320 | tf_op jit(solution)/shard_map/all_gather | solution.py:151
  7.9 6.3 %copy-start.3 = (s32[4]{0:T(128)S(1)}, s32[4]{0:T(128)}, u32[]{:S(2)}) copy-start(s32[4]{0:T(128)} %param.19) | copy-start | bytes 52
  7.9 10.8 %copy-start.1 = (f32[7,2048]{1,0:T(8,128)S(1)}, f32[7,2048]{1,0:T(8,128)}, u32[]{:S(2)}) copy-start(f32[7,2048]{1,0:T(8,128)} %param.13) | copy-start | bytes 172036
  7.9 235.4 %all-gather.5.cloned.1.call-start = ((), (), s32[]{:S(2)}) async-start(), calls=%async_computation.1 | async-start | bytes 7864320 | tf_op jit(solution)/shard_map/all_gather | solution.py:152
  10.5 8.2 %copy-start = (bf16[384,2048]{1,0:T(8,128)(2,1)}, bf16[384,2048]{1,0:T(8,128)(2,1)S(1)}, u32[]{:S(2)}) copy-start(bf16[384,2048]{1,0:T(8,128)(2,1)S(1)} %fusion.61) | copy-start | bytes 4718596
  10.7 28.5 %collective-permute-start = (bf16[127,2048]{1,0:T(8,128)(2,1)S(1)}, bf16[127,2048]{1,0:T(8,128)(2,1)S(1)}, u32[]{:S(2)}, u32[]{:S(2)}) collective-permute-start(bf16[127,2048]{1,0:T(8,128)(2,1)S(1)} %slice.32), channel_id=1, source_target_pairs={{0,4},{4,8},{8,12},{1,5},{5,9},{9,13},{2,6},{6,10},{10,14},{3,7},{... | collective-permute-start | bytes 1560584 | tf_op jit(solution)/shard_map/ppermute | solution.py:14
  41.1 180.2 %copy-start.2 = (f32[2048]{0:T(1024)S(1)}, f32[2048]{0:T(1024)}, u32[]{:S(2)}) copy-start(f32[2048]{0:T(1024)} %param.15) | copy-start | bytes 24580
Sparse Core Ops, SparseCore 0:
  9.6 118.5 all-gather.2
  129.7 113.5 all-gather.4
where the time goes:
time: 313 us; the launch traced here: 306 us
  other arithmetic  198 us (63%)
  matrix products  35.8 us (11%)
  waiting for transfers between devices  30.1 us (10%)
  local copies, waits for them, and re-layouts  22.5 us (7%)
  between operations  16.2 us (5%)
  starting transfers between devices  3.56 us (1%)
    add x16, other arithmetic, tap_block(): partial_value + tap_term(block_index * 8 + offset, medium_filter)  157 us
    dynamic_slice x17, local copies, waits for them, and re-layouts, tap_term(): taps = lax.dynamic_index_in_dim(filter_bank, tap_index, 0, keepdims=False)  21.1 us
    ppermute x1, waiting for transfers between devices, passed_along(): return lax.ppermute(value, axis, pairs)  20.4 us
    dot_general x1, matrix products, compute(): jnp.einsum('rhd,nhd->hrn', query_heads, key_heads, preferred_element_type...  18.3 us
    reduce_sum x1, other arithmetic, compute(): new_total = running_total * rescale + jnp.sum(weights, axis=2)  17.6 us
    dot_general x1, matrix products, compute(): jnp.einsum('hrn,nhd->hrd', weights.astype(jnp.bfloat16), value_heads, pre...  17.6 us
    convert_element_type x1, other arithmetic, hyena_mix(): return mixed.astype(jnp.bfloat16)  13.1 us
    all_gather x1, waiting for transfers between devices, attention_mix(): lax.all_gather(attn_value, 'seq', axis=0, tiled=True)  8.96 us
  transfers between devices with their start and end apart: 3, of which 2 were waited for; matrix products, arithmetic and copies ran while one was open for 65% of the time, Pallas kernels for 0%

commit v1 on v0

--- a/solution.py
+++ b/solution.py
@@ -3,6 +3,8 @@
 import jax
 import jax.numpy as jnp
 from jax import lax
+from jax.experimental import pallas as pl
+from jax.experimental.pallas import tpu as pltpu
 from jax.sharding import PartitionSpec as P
 
 HD = 128
@@ -158,11 +160,322 @@
     return result.transpose(1, 0, 2).reshape(row_count, col_count).astype(jnp.bfloat16)
 
 
+LOG2E = 1.4426950408889634
+LN2 = 0.6931471805599453
+SCALE2 = HD**-0.5 * LOG2E
+NEG = -1e30
+CHUNKS = 4
+STAT_ROWS = 16
+
+
+def hyena_kernel(row_count, rim, lens_ref, ext_in, query_ref, filt_ref, out_ref, ext_ref):
+    base = lens_ref[lens_ref.shape[0] - 1]
+    ext_ref[...] = ext_in[...]
+    taps = filt_ref.shape[0]
+    zero_row = jnp.zeros(ext_ref.shape[1:], ext_ref.dtype)
+    start = jnp.int32(0)
+    for doc in range(lens_ref.shape[0] - 1):
+        end = start + lens_ref[doc]
+        first = jnp.clip(start - base, -rim, row_count)
+        last = jnp.clip(end - base, 0, row_count)
+
+        @pl.when((last > 0) & (first < row_count) & (first < last))
+        def _():
+            def wipe(row, carry):
+                ext_ref[row] = zero_row
+                return carry
+
+            lax.fori_loop(jnp.maximum(first, 0), first + rim, wipe, 0)
+            tile_lo = jnp.maximum(first, 0) // 8
+            tile_hi = (last + 7) // 8
+
+            def tile_body(tile, carry):
+                t0 = pl.multiple_of(tile * 8, 8)
+
+                def tap_body(block, accs):
+                    j0 = pl.multiple_of(block * 8, 8)
+                    fs = [filt_ref[j0 + o] for o in range(8)]
+                    low = t0 + rim - j0 - 7
+                    gs = [ext_ref[low + o] for o in range(15)]
+                    out = []
+                    for i in range(8):
+                        prods = [gs[i + 7 - o] * fs[o] for o in range(8)]
+                        while len(prods) > 1:
+                            prods = [a + b for a, b in zip(prods[::2], prods[1::2])]
+                        out.append(accs[i] + prods[0].astype(jnp.float32))
+                    return tuple(out)
+
+                zeros = jnp.zeros(ext_ref.shape[1:], jnp.float32)
+                accs = lax.fori_loop(0, taps // 8, tap_body, (zeros,) * 8)
+                for i in range(8):
+                    mixed = query_ref[t0 + i].astype(jnp.float32) * accs[i]
+
+                    @pl.when(t0 + i >= first)
+                    def _():
+                        out_ref[t0 + i] = mixed.astype(out_ref.dtype)
+
+                return carry
+
+            lax.fori_loop(tile_lo, tile_hi, tile_body, 0)
+
+        start = end
+
+
+def hyena_fast(features, short_filter, medium_filter, skip_gain, lengths):
+    row_count, _, cols = features.shape
+    taps = medium_filter.shape[0]
+    subs = cols // 128
+    span_index = lax.axis_index("seq")
+    gated = (features[:, 1].astype(jnp.float32) * features[:, 2].astype(jnp.float32)).astype(
+        jnp.bfloat16
+    )
+    carried = passed_along(gated[row_count - taps :], "seq", 1)
+    ext = jnp.concatenate((carried, gated), axis=0).reshape(row_count + taps, subs, 128)
+    query = features[:, 0].reshape(row_count, subs, 128)
+    filt = medium_filter.at[: short_filter.shape[0]].add(short_filter)
+    filt = filt.at[0].add(skip_gain).astype(jnp.bfloat16).reshape(taps, subs, 128)
+    scalars = jnp.concatenate((lengths, jnp.reshape(span_index * row_count, (1,)).astype(jnp.int32)))
+    vmem = pl.BlockSpec(memory_space=pltpu.VMEM)
+    out = pl.pallas_call(
+        lambda *refs: hyena_kernel(row_count, taps, *refs),
+        out_shape=jax.ShapeDtypeStruct((row_count, subs, 128), jnp.bfloat16),
+        in_specs=[pl.BlockSpec(memory_space=pltpu.SMEM), vmem, vmem, vmem],
+        out_specs=vmem,
+        scratch_shapes=[pltpu.VMEM((row_count + taps, subs, 128), jnp.bfloat16)],
+        compiler_params=pltpu.CompilerParams(vmem_limit_bytes=24 * 2**20),
+        cost_estimate=pl.CostEstimate(
+            flops=2 * taps * row_count * cols * 10, bytes_accessed=7 * 2**20, transcendentals=0
+        ),
+        name="hyena",
+    )(scalars, ext, query, filt)
+    return out.reshape(row_count, cols)
+
+
+def doc_start(pos, lens_ref):
+    start = jnp.zeros_like(pos)
+    end = jnp.int32(0)
+    for doc in range(lens_ref.shape[0] - 1):
+        end = end + lens_ref[doc]
+        start = jnp.where(pos >= end, end, start)
+    return start
+
+
+def attn_kernel(rows, lens_ref, q_ref, qa_ref, qb_ref, kp_ref, vp_ref, k_ref, v_ref,
+                o_ref, lse_ref, oa_ref, ob_ref, b00, b10, b01, b11, b02):
+    span = lens_ref[lens_ref.shape[0] - 1]
+    base = span * rows
+
+    def needs(ahead, back):
+        q_first = base + ahead * rows
+        start = jnp.int32(0)
+        end = jnp.int32(0)
+        for doc in range(lens_ref.shape[0] - 1):
+            end = end + lens_ref[doc]
+            start = jnp.where(q_first >= end, end, start)
+        return start < base + (1 - back) * rows
+
+    own_prev = (span == 1) & needs(0, 1)
+    a_here = ((span == 1) | (span == 2)) & needs(1, 0)
+    a_prev = (span == 1) & needs(1, 1)
+    b_here = (span == 1) & needs(2, 0)
+
+    @pl.when(pl.program_id(0) == 0)
+    def _():
+        def fill(ref, ahead, back):
+            qpos = base + ahead * rows + lax.broadcasted_iota(jnp.int32, (rows, 1), 0)
+            starts = doc_start(qpos, lens_ref)
+            kpos = base - back * rows + lax.broadcasted_iota(jnp.int32, (1, rows), 1)
+            ref[...] = jnp.where((kpos <= qpos) & (kpos >= starts), 0.0, NEG).astype(jnp.float32)
+
+        fill(b00, 0, 0)
+        pl.when(own_prev)(lambda: fill(b01, 0, 1))
+        pl.when(a_here)(lambda: fill(b10, 1, 0))
+        pl.when(a_prev)(lambda: fill(b11, 1, 1))
+        pl.when(b_here)(lambda: fill(b02, 2, 0))
+
+    step = 128
+    ones = jnp.ones((rows, 128), jnp.bfloat16)
+
+    def attend(query_ref, keys, values, biases, emit):
+        vals = [jnp.concatenate((v[...], ones), axis=1) for v in values]
+        for r in range(0, rows, step):
+            q = query_ref[r : r + step, :]
+            scores = [
+                lax.dot_general(q, k[...], (((1,), (1,)), ((), ())),
+                                preferred_element_type=jnp.float32) + b[r : r + step, :]
+                for k, b in zip(keys, biases)
+            ]
+            top = jnp.max(scores[0], axis=1, keepdims=True)
+            for s in scores[1:]:
+                top = jnp.maximum(top, jnp.max(s, axis=1, keepdims=True))
+            acc = None
+            for s, v in zip(scores, vals):
+                w = jnp.exp2((s - top) * SCALE2).astype(jnp.bfloat16)
+                part = jnp.dot(w, v, preferred_element_type=jnp.float32)
+                acc = part if acc is None else acc + part
+            total = acc[:, 128:]
+            emit(r, acc[:, :128] / total, top * SCALE2 + jnp.log2(total))
+
+    def emit_own(r, out, lse):
+        o_ref[r : r + step, :] = out
+        lse_ref[r : r + step, :] = lse
+
+    eye = lax.broadcasted_iota(jnp.int32, (128, 128), 0) == lax.broadcasted_iota(
+        jnp.int32, (128, 128), 1
+    )
+    stat_iota = lax.broadcasted_iota(jnp.int32, (STAT_ROWS, 128), 0)
+
+    def emit_to(ref):
+        stats = [jnp.zeros((STAT_ROWS, 128), jnp.float32)]
+
+        def emit(r, out, lse):
+            ref[r : r + step, :] = out.astype(jnp.bfloat16)
+            rest = jnp.sum(jnp.where(eye, lse, 0.0), axis=0, keepdims=True)
+            for piece in range(3):
+                high = rest.astype(jnp.bfloat16).astype(jnp.float32)
+                stats[0] = jnp.where(stat_iota == piece * (rows // step) + r // step, high, stats[0])
+                rest = rest - high
+            if r + step == rows:
+                ref[rows:, :] = stats[0].astype(jnp.bfloat16)
+
+        return emit
+
+    def empty(ref):
+        ref[:rows, :] = jnp.zeros((rows, 128), jnp.bfloat16)
+        ref[rows:, :] = jnp.where(stat_iota < rows // step, NEG, 0.0).astype(jnp.bfloat16)
+
+    pl.when(own_prev)(lambda: attend(q_ref, (kp_ref, k_ref), (vp_ref, v_ref), (b01, b00), emit_own))
+    pl.when(jnp.logical_not(own_prev))(lambda: attend(q_ref, (k_ref,), (v_ref,), (b00,), emit_own))
+    pl.when(a_prev)(
+        lambda: attend(qa_ref, (kp_ref, k_ref), (vp_ref, v_ref), (b11, b10), emit_to(oa_ref))
+    )
+    pl.when(a_here & jnp.logical_not(a_prev))(
+        lambda: attend(qa_ref, (k_ref,), (v_ref,), (b10,), emit_to(oa_ref))
+    )
+    pl.when(jnp.logical_not(a_here))(lambda: empty(oa_ref))
+    pl.when(b_here)(lambda: attend(qb_ref, (k_ref,), (v_ref,), (b02,), emit_to(ob_ref)))
+    pl.when(jnp.logical_not(b_here))(lambda: empty(ob_ref))
+
+
+def merge_kernel(rows, lens_ref, o_ref, lse_ref, ra_ref, rb_ref, out_ref):
+    span = lens_ref[lens_ref.shape[0] - 1]
+    step = 128
+    eye = lax.broadcasted_iota(jnp.int32, (128, 128), 0) == lax.broadcasted_iota(
+        jnp.int32, (128, 128), 1
+    )
+
+    @pl.when(span < 2)
+    def _():
+        out_ref[...] = o_ref[...].astype(jnp.bfloat16)
+
+    @pl.when(span >= 2)
+    def _():
+        blocks = rows // step
+        stat_a = ra_ref[rows:, :].astype(jnp.float32)
+        stat_b = rb_ref[rows:, :].astype(jnp.float32)
+
+        def column(stats, i):
+            row = (stats[i : i + 1] + stats[blocks + i : blocks + i + 1]) + stats[
+                2 * blocks + i : 2 * blocks + i + 1
+            ]
+            return jnp.sum(jnp.where(eye, row, 0.0), axis=1, keepdims=True)
+
+        for i in range(blocks):
+            r = i * step
+            own = lse_ref[r : r + step, :]
+            lse_a = column(stat_a, i)
+            lse_b = jnp.where(span == 3, column(stat_b, i), NEG)
+            top = jnp.maximum(own, jnp.maximum(lse_a, lse_b))
+            w0 = jnp.exp2(own - top)
+            w1 = jnp.exp2(lse_a - top)
+            w2 = jnp.exp2(lse_b - top)
+            total = (
+                o_ref[r : r + step, :] * w0
+                + ra_ref[r : r + step, :].astype(jnp.float32) * w1
+                + rb_ref[r : r + step, :].astype(jnp.float32) * w2
+            )
+            out_ref[r : r + step, :] = (total / (w0 + w1 + w2)).astype(jnp.bfloat16)
+
+
+def attention_fast(attn_query, attn_key, attn_value, lengths):
+    rows, cols = attn_query.shape
+    span_index = lax.axis_index("seq")
+    scalars = jnp.concatenate((lengths, jnp.reshape(span_index, (1,)).astype(jnp.int32)))
+    width = cols // CHUNKS
+    heads = width // HD
+    smem = pl.BlockSpec(memory_space=pltpu.SMEM)
+    block = pl.BlockSpec((rows, HD), lambda h: (0, h))
+    tall = pl.BlockSpec((rows + STAT_ROWS, HD), lambda h: (0, h))
+    sent = []
+    for c in range(CHUNKS):
+        sl = slice(c * width, (c + 1) * width)
+        qc, kc, vc = attn_query[:, sl], attn_key[:, sl], attn_value[:, sl]
+        qa = lax.ppermute(qc, "seq", [(2, 1), (3, 2)])
+        qb = lax.ppermute(qc, "seq", [(3, 1)])
+        kp = lax.ppermute(kc, "seq", [(0, 1)])
+        vp = lax.ppermute(vc, "seq", [(0, 1)])
+        sent.append((qa, qb, kp, vp))
+    outs = []
+    for c in range(CHUNKS):
+        qa, qb, kp, vp = sent[c]
+        first = c * heads
+        whole = pl.BlockSpec((rows, HD), lambda h, first=first: (0, first + h))
+        own, lse, oa, ob = pl.pallas_call(
+            lambda *refs: attn_kernel(rows, *refs),
+            grid=(heads,),
+            out_shape=(
+                jax.ShapeDtypeStruct((rows, width), jnp.float32),
+                jax.ShapeDtypeStruct((rows, width), jnp.float32),
+                jax.ShapeDtypeStruct((rows + STAT_ROWS, width), jnp.bfloat16),
+                jax.ShapeDtypeStruct((rows + STAT_ROWS, width), jnp.bfloat16),
+            ),
+            in_specs=[smem, whole, block, block, block, block, whole, whole],
+            out_specs=(block, block, tall, tall),
+            scratch_shapes=[pltpu.VMEM((rows, rows), jnp.float32)] * 5,
+            compiler_params=pltpu.CompilerParams(vmem_limit_bytes=32 * 2**20),
+            cost_estimate=pl.CostEstimate(
+                flops=heads * 5 * rows * rows * HD * 4 * 2,
+                bytes_accessed=8 * 2**20,
+                transcendentals=heads * 5 * rows * rows,
+            ),
+            name="attend",
+        )(scalars, attn_query, qa, qb, kp, vp, attn_key, attn_value)
+        ra = lax.ppermute(oa, "seq", [(1, 2), (2, 3)])
+        rb = lax.ppermute(ob, "seq", [(1, 3)])
+        outs.append((own, lse, ra, rb))
+    merged = []
+    for own, lse, ra, rb in outs:
+        merged.append(
+            pl.pallas_call(
+                lambda *refs: merge_kernel(rows, *refs),
+                grid=(heads,),
+                out_shape=jax.ShapeDtypeStruct((rows, width), jnp.bfloat16),
+                in_specs=[smem, block, block, tall, tall],
+                out_specs=block,
+                cost_estimate=pl.CostEstimate(
+                    flops=rows * width * 16, bytes_accessed=6 * 2**20, transcendentals=0
+                ),
+                name="merge",
+            )(scalars, own, lse, ra, rb)
+        )
+    return jnp.concatenate(merged, axis=1)
+
+
 def local(
     features, short_filter, medium_filter, skip_gain, attn_query, attn_key, attn_value, lengths
 ):
-    hyena_out = hyena_mix(features, short_filter, medium_filter, skip_gain, lengths)
-    attn_out = attention_mix(attn_query, attn_key, attn_value, lengths)
+    rows, cols = attn_query.shape
+    spans = lax.axis_size("seq")
+    if cols % 2048 == 0 and rows % 8 == 0:
+        hyena = hyena_fast
+    else:
+        hyena = hyena_mix
+    if spans == 4 and rows % 128 == 0 and rows <= 640 and cols % (CHUNKS * HD) == 0:
+        attention = attention_fast
+    else:
+        attention = attention_mix
+    hyena_out = hyena(features, short_filter, medium_filter, skip_gain, lengths)
+    attn_out = attention(attn_query, attn_key, attn_value, lengths)
     return (hyena_out, attn_out)
 
 

time: 313 us -> 192 us (0.61); the launches traced: 306 us -> 191 us
  other arithmetic: 198 us -> 5.1 us
  Pallas kernels: 0 us -> 79.5 us
  starting transfers between devices: 3.56 us -> 44.1 us
  matrix products: 35.8 us -> 0 us
  between operations: 16.2 us -> 1.31 us
  waiting for transfers between devices: 30.1 us -> 38.4 us
    add x18 -> x2, other arithmetic: 157 us -> 0.02 us  [the longest x1 0.01 us: hyena_fast(): filt.at[0].add(skip_gain).astype(jnp.bfloat16).reshape(taps, subs, 128)]
    pallas_call x0 -> x9, Pallas kernels: none -> 79.5 us  [the longest x1 39.9 us: hyena_fast(): pl.pallas_call(lambda *refs: hyena_kernel(row_count, taps, *refs), out_sh...]
    ppermute x0 -> x24, starting transfers between devices: none -> 42.2 us  [the longest x4 12.6 us: attention_fast(): rb = lax.ppermute(ob, 'seq', [(1, 3)])]
    ppermute x0 -> x24, waiting for transfers between devices: none -> 38.4 us  [the longest x4 11.8 us: attention_fast(): vp = lax.ppermute(vc, 'seq', [(0, 1)])]
    dot_general x2 -> x0, matrix products: 35.8 us -> none  [the longest x1 18.3 us: compute(): jnp.einsum('rhd,nhd->hrn', query_heads, key_heads, preferred_element_type...]
    dynamic_slice x18 -> x0, local copies, waits for them, and re-layouts: 21.1 us -> none  [the longest x17 21.1 us: tap_term(): taps = lax.dynamic_index_in_dim(filter_bank, tap_index, 0, keepdims=False)]
    ppermute x1, waiting for transfers between devices: 20.4 us -> 0.01 us  [passed_along(): return lax.ppermute(value, axis, pairs)]
    reduce_sum x5 -> x0, other arithmetic: 18.6 us -> none  [the longest x1 17.6 us: compute(): new_total = running_total * rescale + jnp.sum(weights, axis=2)]
  transfers between devices with their start and end apart: 3 -> 25, of which waited for: 2 -> 7; matrix products, arithmetic and copies ran while one was open for 65% -> 7% of each run, Pallas kernels for 0% -> 40%
where the time goes in v1:
time: 192 us; the launch traced here: 191 us
  Pallas kernels  79.5 us (41%)
  starting transfers between devices  44.1 us (23%)
  waiting for transfers between devices  38.4 us (20%)
  local copies, waits for them, and re-layouts  22.4 us (12%)
  other arithmetic  5.1 us (3%)
    pallas_call x1, Pallas kernels, hyena_fast(): pl.pallas_call(lambda *refs: hyena_kernel(row_count, taps, *refs), out_sh...  39.9 us
    pallas_call x4, Pallas kernels, attention_fast(): pl.pallas_call(lambda *refs: attn_kernel(rows, *refs), grid=(heads,), out...  25.1 us
    unnamed x82, local copies, waits for them, and re-layouts  14.9 us
    pallas_call x4, Pallas kernels, attention_fast(): pl.pallas_call(lambda *refs: merge_kernel(rows, *refs), grid=(heads,), ou...  14.4 us
    ppermute x4, starting transfers between devices, attention_fast(): rb = lax.ppermute(ob, 'seq', [(1, 3)])  12.6 us
    ppermute x4, waiting for transfers between devices, attention_fast(): vp = lax.ppermute(vc, 'seq', [(0, 1)])  11.8 us
    ppermute x4, waiting for transfers between devices, attention_fast(): qa = lax.ppermute(qc, 'seq', [(2, 1), (3, 2)])  9.08 us
    ppermute x4, starting transfers between devices, attention_fast(): ra = lax.ppermute(oa, 'seq', [(1, 2), (2, 3)])  8.23 us
  transfers between devices with their start and end apart: 25, of which 7 were waited for; matrix products, arithmetic and copies ran while one was open for 7% of the time, Pallas kernels for 40%

profile of v1, /device:TPU:10, one launch (start us, length us, event | category | flops | bytes accessed | tf_op | source)
XLA Modules:
  0.0 190.8 jit_solution(17428082472471241890)
XLA Ops:
  12.4 1.8 fusion.3
  16.2 9.1 %collective-permute-done.1.refs_2_ = bf16[384,512]{1,0:T(8,128)(2,1)S(1)} collective-permute-done((bf16[384,512]{1,0:T(8,128)(2,1)}, bf16[384,512]{1,0:T(8,128)(2,1)S(1)}, u32[]{:S(2)}, u32[]{:S(2)}) %collective-permute-start.1) | collective-permute-done | bytes 393248 | tf_op jit(solution)/shard_map/ppermute | solution.py:413
  27.3 1.6 scatter-add.6
  33.0 6.2 %collective-permute-done.4.refs_5_ = bf16[384,512]{1,0:T(8,128)(2,1)} collective-permute-done((bf16[384,512]{1,0:T(8,128)(2,1)}, bf16[384,512]{1,0:T(8,128)(2,1)}, u32[]{:S(2)}, u32[]{:S(2)}) %collective-permute-start.4) | collective-permute-done | bytes 393248 | tf_op jit(solution)/shard_map/ppermute | solution.py:416
  45.8 5.5 %collective-permute-done.10.refs_5_ = bf16[384,512]{1,0:T(8,128)(2,1)S(1)} collective-permute-done((bf16[384,512]{1,0:T(8,128)(2,1)}, bf16[384,512]{1,0:T(8,128)(2,1)S(1)}, u32[]{:S(2)}, u32[]{:S(2)}) %collective-permute-start.10) | collective-permute-done | bytes 393248 | tf_op jit(solution)/shard_map/ppermute | solution.py:416
  52.6 7.1 %collective-permute-done.9.refs_4_ = bf16[384,512]{1,0:T(8,128)(2,1)S(1)} collective-permute-done((bf16[384,512]{1,0:T(8,128)(2,1)}, bf16[384,512]{1,0:T(8,128)(2,1)S(1)}, u32[]{:S(2)}, u32[]{:S(2)}) %collective-permute-start.9) | collective-permute-done | bytes 393248 | tf_op jit(solution)/shard_map/ppermute | solution.py:415
  63.7 6.0 %attend.4 = (f32[384,512]{1,0:T(8,128)S(1)}, f32[384,512]{1,0:T(8,128)S(1)}, bf16[400,512]{1,0:T(8,128)(2,1)S(1)}, bf16[400,512]{1,0:T(8,128)(2,1)S(1)}) custom-call(s32[5]{0:T(128)S(1)} %get-tuple-element.70.refs_0_, bf16[384,2048]{1,0:T(8,128)(2,1)S(1)} %copy-done, bf16[384,512]{1,0:T(8,128)(2,1)S(1)} %copy-done.14, ...), custom_call_target="tpu_custom_call" | custom-call | flops 3019898880 | bytes 8388608 | tf_op jit(solution)/shard_map/attend/pallas_call | solution.py:423
  72.9 6.5 %attend.5 = (f32[384,512]{1,0:T(8,128)S(1)}, f32[384,512]{1,0:T(8,128)S(1)}, bf16[400,512]{1,0:T(8,128)(2,1)S(1)}, bf16[400,512]{1,0:T(8,128)(2,1)}) custom-call(s32[5]{0:T(128)S(1)} %get-tuple-element.70.refs_0_, bf16[384,2048]{1,0:T(8,128)(2,1)S(1)} %copy-done, bf16[384,512]{1,0:T(8,128)(2,1)S(1)} %collective-permute-done.7.refs_2_, ...), custom_call_target="tpu_custom_call" | custom-call | flops 3019898880 | bytes 8388608 | tf_op jit(solution)/shard_map/attend/pallas_call | solution.py:423
  81.2 1.9 %collective-permute-start = (bf16[128,2048]{1,0:T(8,128)(2,1)S(1)}, bf16[128,2048]{1,0:T(8,128)(2,1)S(1)}, u32[]{:S(2)}, u32[]{:S(2)}) collective-permute-start(bf16[128,2048]{1,0:T(8,128)(2,1)S(1)} %copy-done.22), channel_id=1, source_target_pairs={{0,4},{4,8},{8,12},{1,5},{5,9},{9,13},{2,6},{6,10},{10,14},{3,7},{... | collective-permute-start | bytes 1572872 | tf_op jit(solution)/shard_map/ppermute | solution.py:16
  83.2 1.7 collective-permute-start.5
  87.8 6.3 %attend.6 = (f32[384,512]{1,0:T(8,128)S(1)}, f32[384,512]{1,0:T(8,128)S(1)}, bf16[400,512]{1,0:T(8,128)(2,1)}, bf16[400,512]{1,0:T(8,128)(2,1)}) custom-call(s32[5]{0:T(128)S(1)} %get-tuple-element.70.refs_0_, bf16[384,2048]{1,0:T(8,128)(2,1)S(1)} %copy-done, bf16[384,512]{1,0:T(8,128)(2,1)S(1)} %collective-permute-done.13.refs_2_, ...), custom_call_target="tpu_custom_call" | custom-call | flops 3019898880 | bytes 8388608 | tf_op jit(solution)/shard_map/attend/pallas_call | solution.py:423
  95.8 2.2 %collective-permute-start.12 = (bf16[400,512]{1,0:T(8,128)(2,1)}, bf16[400,512]{1,0:T(8,128)(2,1)}, u32[]{:S(2)}, u32[]{:S(2)}) collective-permute-start(bf16[400,512]{1,0:T(8,128)(2,1)} %get-tuple-element.49), channel_id=1, source_target_pairs={{4,12},{5,13},{6,14},{7,15},{20,28},{21,29},{22,30},{23,31}} | collective-permute-start | bytes 1228808 | tf_op jit(solution)/shard_map/ppermute | solution.py:444
  98.0 6.3 %attend.7 = (f32[384,512]{1,0:T(8,128)S(1)}, f32[384,512]{1,0:T(8,128)S(1)}, bf16[400,512]{1,0:T(8,128)(2,1)}, bf16[400,512]{1,0:T(8,128)(2,1)}) custom-call(s32[5]{0:T(128)S(1)} %get-tuple-element.70.refs_0_, bf16[384,2048]{1,0:T(8,128)(2,1)S(1)} %copy-done, bf16[384,512]{1,0:T(8,128)(2,1)S(1)} %collective-permute-done.19.refs_2_, ...), custom_call_target="tpu_custom_call" | custom-call | flops 3019898880 | bytes 8388608 | tf_op jit(solution)/shard_map/attend/pallas_call | solution.py:423
  104.3 3.7 %collective-permute-start.17 = (bf16[400,512]{1,0:T(8,128)(2,1)}, bf16[400,512]{1,0:T(8,128)(2,1)S(1)}, u32[]{:S(2)}, u32[]{:S(2)}) collective-permute-start(bf16[400,512]{1,0:T(8,128)(2,1)} %get-tuple-element.52), channel_id=1, source_target_pairs={{4,8},{8,12},{5,9},{9,13},{6,10},{10,14},{7,11},{11,15},{20,24},{2... | collective-permute-start | bytes 1228808 | tf_op jit(solution)/shard_map/ppermute | solution.py:443
  108.0 2.7 %collective-permute-start.18 = (bf16[400,512]{1,0:T(8,128)(2,1)}, bf16[400,512]{1,0:T(8,128)(2,1)S(1)}, u32[]{:S(2)}, u32[]{:S(2)}) collective-permute-start(bf16[400,512]{1,0:T(8,128)(2,1)} %get-tuple-element.53), channel_id=1, source_target_pairs={{4,12},{5,13},{6,14},{7,15},{20,28},{21,29},{22,30},{23,31}} | collective-permute-start | bytes 1228808 | tf_op jit(solution)/shard_map/ppermute | solution.py:444
  110.7 2.4 %collective-permute-done.6.refs_4_ = bf16[400,512]{1,0:T(8,128)(2,1)S(1)} collective-permute-done((bf16[400,512]{1,0:T(8,128)(2,1)S(1)}, bf16[400,512]{1,0:T(8,128)(2,1)S(1)}, u32[]{:S(2)}, u32[]{:S(2)}) %collective-permute-start.6) | collective-permute-done | bytes 409632 | tf_op jit(solution)/shard_map/ppermute | solution.py:444
  114.4 7.5 %collective-permute-done.11.refs_3_ = bf16[400,512]{1,0:T(8,128)(2,1)S(1)} collective-permute-done((bf16[400,512]{1,0:T(8,128)(2,1)S(1)}, bf16[400,512]{1,0:T(8,128)(2,1)S(1)}, u32[]{:S(2)}, u32[]{:S(2)}) %collective-permute-start.11) | collective-permute-done | bytes 409632 | tf_op jit(solution)/shard_map/ppermute | solution.py:443
  121.8 6.4 %collective-permute-start.24 = (bf16[400,512]{1,0:T(8,128)(2,1)}, bf16[400,512]{1,0:T(8,128)(2,1)S(1)}, u32[]{:S(2)}, u32[]{:S(2)}) collective-permute-start(bf16[400,512]{1,0:T(8,128)(2,1)} %get-tuple-element.57), channel_id=1, source_target_pairs={{4,12},{5,13},{6,14},{7,15},{20,28},{21,29},{22,30},{23,31}} | collective-permute-start | bytes 1228808 | tf_op jit(solution)/shard_map/ppermute | solution.py:444
  130.7 39.9 %hyena.1 = bf16[384,16,128]{2,1,0:T(8,128)(2,1)S(1)} custom-call(s32[5]{0:T(128)S(1)} %get-tuple-element.71.refs_0_, bf16[512,16,128]{2,1,0:T(8,128)(2,1)S(1)} %bitcast.22, bf16[384,16,128]{2,1,0:T(8,128)(2,1)S(1)} %bitcast.23, bf16[128,16,128]{2,1,0:T(8,128)(2,1)S(1)} %bitcast.25), custom_call_target="tpu_custom_call" | custom-call | flops 2013265920 | bytes 7340032 | tf_op jit(solution)/shard_map/hyena/pallas_call | solution.py:239
  172.2 3.6 %merge.4 = bf16[384,512]{1,0:T(8,128)(2,1)} custom-call(s32[5]{0:T(128)} %copy-done.12, f32[384,512]{1,0:T(8,128)} %copy-done.4, f32[384,512]{1,0:T(8,128)} %copy-done.5, bf16[400,512]{1,0:T(8,128)(2,1)} %copy-done.23, bf16[400,512]{1,0:T(8,128)(2,1)} %copy-done.25), custom_call_target="tpu_custom_call" | custom-call | flops 3145728 | bytes 6291456 | tf_op jit(solution)/shard_map/merge/pallas_call | solution.py:449
  175.8 3.6 %merge.5 = bf16[384,512]{1,0:T(8,128)(2,1)} custom-call(s32[5]{0:T(128)} %copy-done.12, f32[384,512]{1,0:T(8,128)} %copy-done.6, f32[384,512]{1,0:T(8,128)} %copy-done.7, bf16[400,512]{1,0:T(8,128)(2,1)} %copy-done.24, bf16[400,512]{1,0:T(8,128)(2,1)} %collective-permute-done.12.refs_4_), custom_call_target="tpu_custom_call" | custom-call | flops 3145728 | bytes 6291456 | tf_op jit(solution)/shard_map/merge/pallas_call | solution.py:449
  180.3 3.6 %merge.6 = bf16[384,512]{1,0:T(8,128)(2,1)} custom-call(s32[5]{0:T(128)} %copy-done.12, f32[384,512]{1,0:T(8,128)} %copy-done.8, f32[384,512]{1,0:T(8,128)} %copy-done.9, bf16[400,512]{1,0:T(8,128)(2,1)} %copy-done.26, bf16[400,512]{1,0:T(8,128)(2,1)} %copy-done.28), custom_call_target="tpu_custom_call" | custom-call | flops 3145728 | bytes 6291456 | tf_op jit(solution)/shard_map/merge/pallas_call | solution.py:449
  184.9 3.6 %merge.7 = bf16[384,512]{1,0:T(8,128)(2,1)} custom-call(s32[5]{0:T(128)} %copy-done.12, f32[384,512]{1,0:T(8,128)} %copy-done.10, f32[384,512]{1,0:T(8,128)} %copy-done.11, bf16[400,512]{1,0:T(8,128)(2,1)} %copy-done.27, bf16[400,512]{1,0:T(8,128)(2,1)} %copy-done.29), custom_call_target="tpu_custom_call" | custom-call | flops 3145728 | bytes 6291456 | tf_op jit(solution)/shard_map/merge/pallas_call | solution.py:449
  188.5 2.4 %pad_maximum_fusion = bf16[384,2048]{1,0:T(8,128)(2,1)} fusion(bf16[384,512]{1,0:T(8,128)(2,1)} %merge.7, bf16[384,512]{1,0:T(8,128)(2,1)S(1)} %copy-done.21, bf16[384,512]{1,0:T(8,128)(2,1)S(1)} %copy-done.20, bf16[384,512]{1,0:T(8,128)(2,1)S(1)} %copy-done.19), kind=kLoop, calls=%fused_computation.3 | loop fusion | flops 6291456 | bytes 3145728 | tf_op jit(solution)/shard_map/concatenate | solution.py:461
  (131 shorter events, 48.0 us)
Async XLA Ops:
  3.5 21.7 %collective-permute-start.1 = (bf16[384,512]{1,0:T(8,128)(2,1)}, bf16[384,512]{1,0:T(8,128)(2,1)S(1)}, u32[]{:S(2)}, u32[]{:S(2)}) collective-permute-start(bf16[384,512]{1,0:T(8,128)(2,1)} %get-tuple-element.66), channel_id=1, source_target_pairs={{8,4},{12,8},{9,5},{13,9},{10,6},{14,10},{11,7},{15,11},{24,20},{2... | collective-permute-start | bytes 1179656 | tf_op jit(solution)/shard_map/ppermute | solution.py:413
  5.1 25.3 %collective-permute-start.2 = (bf16[384,512]{1,0:T(8,128)(2,1)}, bf16[384,512]{1,0:T(8,128)(2,1)}, u32[]{:S(2)}, u32[]{:S(2)}) collective-permute-start(bf16[384,512]{1,0:T(8,128)(2,1)} %get-tuple-element.66), channel_id=1, source_target_pairs={{12,4},{13,5},{14,6},{15,7},{28,20},{29,21},{30,22},{31,23}} | collective-permute-start | bytes 1179656 | tf_op jit(solution)/shard_map/ppermute | solution.py:414
  6.5 34.0 %collective-permute-start.7 = (bf16[384,512]{1,0:T(8,128)(2,1)}, bf16[384,512]{1,0:T(8,128)(2,1)S(1)}, u32[]{:S(2)}, u32[]{:S(2)}) collective-permute-start(bf16[384,512]{1,0:T(8,128)(2,1)} %get-tuple-element.68), channel_id=1, source_target_pairs={{8,4},{12,8},{9,5},{13,9},{10,6},{14,10},{11,7},{15,11},{24,20},{2... | collective-permute-start | bytes 1179656 | tf_op jit(solution)/shard_map/ppermute | solution.py:413
  7.8 36.6 %collective-permute-start.8 = (bf16[384,512]{1,0:T(8,128)(2,1)}, bf16[384,512]{1,0:T(8,128)(2,1)}, u32[]{:S(2)}, u32[]{:S(2)}) collective-permute-start(bf16[384,512]{1,0:T(8,128)(2,1)} %get-tuple-element.68), channel_id=1, source_target_pairs={{12,4},{13,5},{14,6},{15,7},{28,20},{29,21},{30,22},{31,23}} | collective-permute-start | bytes 1179656 | tf_op jit(solution)/shard_map/ppermute | solution.py:414
  10.4 21.4 %collective-permute-start.3 = (bf16[384,512]{1,0:T(8,128)(2,1)}, bf16[384,512]{1,0:T(8,128)(2,1)}, u32[]{:S(2)}, u32[]{:S(2)}) collective-permute-start(bf16[384,512]{1,0:T(8,128)(2,1)} %get-tuple-element.62), channel_id=1, source_target_pairs={{0,4},{1,5},{2,6},{3,7},{16,20},{17,21},{18,22},{19,23}} | collective-permute-start | bytes 1179656 | tf_op jit(solution)/shard_map/ppermute | solution.py:415
  26.0 13.3 %collective-permute-start.4 = (bf16[384,512]{1,0:T(8,128)(2,1)}, bf16[384,512]{1,0:T(8,128)(2,1)}, u32[]{:S(2)}, u32[]{:S(2)}) collective-permute-start(bf16[384,512]{1,0:T(8,128)(2,1)} %get-tuple-element.58), channel_id=1, source_target_pairs={{0,4},{1,5},{2,6},{3,7},{16,20},{17,21},{18,22},{19,23}} | collective-permute-start | bytes 1179656 | tf_op jit(solution)/shard_map/ppermute | solution.py:416
  30.4 30.6 %collective-permute-start.13 = (bf16[384,512]{1,0:T(8,128)(2,1)}, bf16[384,512]{1,0:T(8,128)(2,1)S(1)}, u32[]{:S(2)}, u32[]{:S(2)}) collective-permute-start(bf16[384,512]{1,0:T(8,128)(2,1)} %get-tuple-element.67), channel_id=1, source_target_pairs={{8,4},{12,8},{9,5},{13,9},{10,6},{14,10},{11,7},{15,11},{24,20},{2... | collective-permute-start | bytes 1179656 | tf_op jit(solution)/shard_map/ppermute | solution.py:413
  31.7 30.6 %collective-permute-start.14 = (bf16[384,512]{1,0:T(8,128)(2,1)}, bf16[384,512]{1,0:T(8,128)(2,1)S(1)}, u32[]{:S(2)}, u32[]{:S(2)}) collective-permute-start(bf16[384,512]{1,0:T(8,128)(2,1)} %get-tuple-element.67), channel_id=1, source_target_pairs={{12,4},{13,5},{14,6},{15,7},{28,20},{29,21},{30,22},{31,23}} | collective-permute-start | bytes 1179656 | tf_op jit(solution)/shard_map/ppermute | solution.py:414
  40.6 19.1 %collective-permute-start.9 = (bf16[384,512]{1,0:T(8,128)(2,1)}, bf16[384,512]{1,0:T(8,128)(2,1)S(1)}, u32[]{:S(2)}, u32[]{:S(2)}) collective-permute-start(bf16[384,512]{1,0:T(8,128)(2,1)} %get-tuple-element.64), channel_id=1, source_target_pairs={{0,4},{1,5},{2,6},{3,7},{16,20},{17,21},{18,22},{19,23}} | collective-permute-start | bytes 1179656 | tf_op jit(solution)/shard_map/ppermute | solution.py:415
  44.4 27.1 %collective-permute-start.15 = (bf16[384,512]{1,0:T(8,128)(2,1)}, bf16[384,512]{1,0:T(8,128)(2,1)S(1)}, u32[]{:S(2)}, u32[]{:S(2)}) collective-permute-start(bf16[384,512]{1,0:T(8,128)(2,1)} %get-tuple-element.63), channel_id=1, source_target_pairs={{0,4},{1,5},{2,6},{3,7},{16,20},{17,21},{18,22},{19,23}} | collective-permute-start | bytes 1179656 | tf_op jit(solution)/shard_map/ppermute | solution.py:415
  51.3 31.8 %collective-permute-start.19 = (bf16[384,512]{1,0:T(8,128)(2,1)S(1)}, bf16[384,512]{1,0:T(8,128)(2,1)S(1)}, u32[]{:S(2)}, u32[]{:S(2)}) collective-permute-start(bf16[384,512]{1,0:T(8,128)(2,1)S(1)} %copy-done.30), channel_id=1, source_target_pairs={{8,4},{12,8},{9,5},{13,9},{10,6},{14,10},{11,7},{15,11},{24,20},{2... | collective-permute-start | bytes 1179656 | tf_op jit(solution)/shard_map/ppermute | solution.py:413
  59.7 25.2 %collective-permute-start.20 = (bf16[384,512]{1,0:T(8,128)(2,1)S(1)}, bf16[384,512]{1,0:T(8,128)(2,1)S(1)}, u32[]{:S(2)}, u32[]{:S(2)}) collective-permute-start(bf16[384,512]{1,0:T(8,128)(2,1)S(1)} %copy-done.30), channel_id=1, source_target_pairs={{12,4},{13,5},{14,6},{15,7},{28,20},{29,21},{30,22},{31,23}} | collective-permute-start | bytes 1179656 | tf_op jit(solution)/shard_map/ppermute | solution.py:414
  61.0 20.2 %collective-permute-start.16 = (bf16[384,512]{1,0:T(8,128)(2,1)S(1)}, bf16[384,512]{1,0:T(8,128)(2,1)S(1)}, u32[]{:S(2)}, u32[]{:S(2)}) collective-permute-start(bf16[384,512]{1,0:T(8,128)(2,1)S(1)} %copy-done.33), channel_id=1, source_target_pairs={{0,4},{1,5},{2,6},{3,7},{16,20},{17,21},{18,22},{19,23}} | collective-permute-start | bytes 1179656 | tf_op jit(solution)/shard_map/ppermute | solution.py:416
  62.4 23.9 %collective-permute-start.21 = (bf16[384,512]{1,0:T(8,128)(2,1)S(1)}, bf16[384,512]{1,0:T(8,128)(2,1)S(1)}, u32[]{:S(2)}, u32[]{:S(2)}) collective-permute-start(bf16[384,512]{1,0:T(8,128)(2,1)S(1)} %copy-done.32), channel_id=1, source_target_pairs={{0,4},{1,5},{2,6},{3,7},{16,20},{17,21},{18,22},{19,23}} | collective-permute-start | bytes 1179656 | tf_op jit(solution)/shard_map/ppermute | solution.py:415
  71.5 24.4 %collective-permute-start.22 = (bf16[384,512]{1,0:T(8,128)(2,1)S(1)}, bf16[384,512]{1,0:T(8,128)(2,1)S(1)}, u32[]{:S(2)}, u32[]{:S(2)}) collective-permute-start(bf16[384,512]{1,0:T(8,128)(2,1)S(1)} %copy-done.31), channel_id=1, source_target_pairs={{0,4},{1,5},{2,6},{3,7},{16,20},{17,21},{18,22},{19,23}} | collective-permute-start | bytes 1179656 | tf_op jit(solution)/shard_map/ppermute | solution.py:416
  81.2 23.1 %collective-permute-start = (bf16[128,2048]{1,0:T(8,128)(2,1)S(1)}, bf16[128,2048]{1,0:T(8,128)(2,1)S(1)}, u32[]{:S(2)}, u32[]{:S(2)}) collective-permute-start(bf16[128,2048]{1,0:T(8,128)(2,1)S(1)} %copy-done.22), channel_id=1, source_target_pairs={{0,4},{4,8},{8,12},{1,5},{5,9},{9,13},{2,6},{6,10},{10,14},{3,7},{... | collective-permute-start | bytes 1572872 | tf_op jit(solution)/shard_map/ppermute | solution.py:16
  83.2 24.8 %collective-permute-start.5 = (bf16[400,512]{1,0:T(8,128)(2,1)S(1)}, bf16[400,512]{1,0:T(8,128)(2,1)S(1)}, u32[]{:S(2)}, u32[]{:S(2)}) collective-permute-start(bf16[400,512]{1,0:T(8,128)(2,1)S(1)} %get-tuple-element.44), channel_id=1, source_target_pairs={{4,8},{8,12},{5,9},{9,13},{6,10},{10,14},{7,11},{11,15},{20,24},{2... | collective-permute-start | bytes 1228808 | tf_op jit(solution)/shard_map/ppermute | solution.py:443
  84.9 28.1 %collective-permute-start.6 = (bf16[400,512]{1,0:T(8,128)(2,1)S(1)}, bf16[400,512]{1,0:T(8,128)(2,1)S(1)}, u32[]{:S(2)}, u32[]{:S(2)}) collective-permute-start(bf16[400,512]{1,0:T(8,128)(2,1)S(1)} %get-tuple-element.45), channel_id=1, source_target_pairs={{4,12},{5,13},{6,14},{7,15},{20,28},{21,29},{22,30},{23,31}} | collective-permute-start | bytes 1228808 | tf_op jit(solution)/shard_map/ppermute | solution.py:444
  86.2 35.6 %collective-permute-start.11 = (bf16[400,512]{1,0:T(8,128)(2,1)S(1)}, bf16[400,512]{1,0:T(8,128)(2,1)S(1)}, u32[]{:S(2)}, u32[]{:S(2)}) collective-permute-start(bf16[400,512]{1,0:T(8,128)(2,1)S(1)} %get-tuple-element.48), channel_id=1, source_target_pairs={{4,8},{8,12},{5,9},{9,13},{6,10},{10,14},{7,11},{11,15},{20,24},{2... | collective-permute-start | bytes 1228808 | tf_op jit(solution)/shard_map/ppermute | solution.py:443
  95.8 80.0 %collective-permute-start.12 = (bf16[400,512]{1,0:T(8,128)(2,1)}, bf16[400,512]{1,0:T(8,128)(2,1)}, u32[]{:S(2)}, u32[]{:S(2)}) collective-permute-start(bf16[400,512]{1,0:T(8,128)(2,1)} %get-tuple-element.49), channel_id=1, source_target_pairs={{4,12},{5,13},{6,14},{7,15},{20,28},{21,29},{22,30},{23,31}} | collective-permute-start | bytes 1228808 | tf_op jit(solution)/shard_map/ppermute | solution.py:444
  104.3 75.2 %collective-permute-start.17 = (bf16[400,512]{1,0:T(8,128)(2,1)}, bf16[400,512]{1,0:T(8,128)(2,1)S(1)}, u32[]{:S(2)}, u32[]{:S(2)}) collective-permute-start(bf16[400,512]{1,0:T(8,128)(2,1)} %get-tuple-element.52), channel_id=1, source_target_pairs={{4,8},{8,12},{5,9},{9,13},{6,10},{10,14},{7,11},{11,15},{20,24},{2... | collective-permute-start | bytes 1228808 | tf_op jit(solution)/shard_map/ppermute | solution.py:443
  108.0 71.5 %collective-permute-start.18 = (bf16[400,512]{1,0:T(8,128)(2,1)}, bf16[400,512]{1,0:T(8,128)(2,1)S(1)}, u32[]{:S(2)}, u32[]{:S(2)}) collective-permute-start(bf16[400,512]{1,0:T(8,128)(2,1)} %get-tuple-element.53), channel_id=1, source_target_pairs={{4,12},{5,13},{6,14},{7,15},{20,28},{21,29},{22,30},{23,31}} | collective-permute-start | bytes 1228808 | tf_op jit(solution)/shard_map/ppermute | solution.py:444
  113.1 70.9 %collective-permute-start.23 = (bf16[400,512]{1,0:T(8,128)(2,1)}, bf16[400,512]{1,0:T(8,128)(2,1)S(1)}, u32[]{:S(2)}, u32[]{:S(2)}) collective-permute-start(bf16[400,512]{1,0:T(8,128)(2,1)} %get-tuple-element.56), channel_id=1, source_target_pairs={{4,8},{8,12},{5,9},{9,13},{6,10},{10,14},{7,11},{11,15},{20,24},{2... | collective-permute-start | bytes 1228808 | tf_op jit(solution)/shard_map/ppermute | solution.py:443
  121.8 62.1 %collective-permute-start.24 = (bf16[400,512]{1,0:T(8,128)(2,1)}, bf16[400,512]{1,0:T(8,128)(2,1)S(1)}, u32[]{:S(2)}, u32[]{:S(2)}) collective-permute-start(bf16[400,512]{1,0:T(8,128)(2,1)} %get-tuple-element.57), channel_id=1, source_target_pairs={{4,12},{5,13},{6,14},{7,15},{20,28},{21,29},{22,30},{23,31}} | collective-permute-start | bytes 1228808 | tf_op jit(solution)/shard_map/ppermute | solution.py:444
  (39 other events, 395.7 us)

commit v2 on v1

--- a/solution.py
+++ b/solution.py
@@ -2,6 +2,7 @@
 
 import jax
 import jax.numpy as jnp
+import numpy as np
 from jax import lax
 from jax.experimental import pallas as pl
 from jax.experimental.pallas import tpu as pltpu
@@ -164,91 +165,107 @@
 LN2 = 0.6931471805599453
 SCALE2 = HD**-0.5 * LOG2E
 NEG = -1e30
-CHUNKS = 4
+CHUNKS = 2
 STAT_ROWS = 16
 
 
-def hyena_kernel(row_count, rim, lens_ref, ext_in, query_ref, filt_ref, out_ref, ext_ref):
+def hyena_kernel(row_count, taps, lens_ref, feat_ref, rim_ref, filt_ref, fwd_ref, inv_ref, out_ref,
+                 ext_ref, sum_ref):
     base = lens_ref[lens_ref.shape[0] - 1]
-    ext_ref[...] = ext_in[...]
-    taps = filt_ref.shape[0]
-    zero_row = jnp.zeros(ext_ref.shape[1:], ext_ref.dtype)
-    start = jnp.int32(0)
-    for doc in range(lens_ref.shape[0] - 1):
-        end = start + lens_ref[doc]
-        first = jnp.clip(start - base, -rim, row_count)
-        last = jnp.clip(end - base, 0, row_count)
-
-        @pl.when((last > 0) & (first < row_count) & (first < last))
-        def _():
-            def wipe(row, carry):
-                ext_ref[row] = zero_row
-                return carry
-
-            lax.fori_loop(jnp.maximum(first, 0), first + rim, wipe, 0)
-            tile_lo = jnp.maximum(first, 0) // 8
-            tile_hi = (last + 7) // 8
-
-            def tile_body(tile, carry):
-                t0 = pl.multiple_of(tile * 8, 8)
-
-                def tap_body(block, accs):
-                    j0 = pl.multiple_of(block * 8, 8)
-                    fs = [filt_ref[j0 + o] for o in range(8)]
-                    low = t0 + rim - j0 - 7
-                    gs = [ext_ref[low + o] for o in range(15)]
-                    out = []
-                    for i in range(8):
-                        prods = [gs[i + 7 - o] * fs[o] for o in range(8)]
-                        while len(prods) > 1:
-                            prods = [a + b for a, b in zip(prods[::2], prods[1::2])]
-                        out.append(accs[i] + prods[0].astype(jnp.float32))
-                    return tuple(out)
-
-                zeros = jnp.zeros(ext_ref.shape[1:], jnp.float32)
-                accs = lax.fori_loop(0, taps // 8, tap_body, (zeros,) * 8)
-                for i in range(8):
-                    mixed = query_ref[t0 + i].astype(jnp.float32) * accs[i]
-
-                    @pl.when(t0 + i >= first)
-                    def _():
-                        out_ref[t0 + i] = mixed.astype(out_ref.dtype)
-
-                return carry
-
-            lax.fori_loop(tile_lo, tile_hi, tile_body, 0)
-
-        start = end
+    ext_ref[:taps, :] = rim_ref[...]
+    ext_ref[taps:, :] = (
+        feat_ref[1].astype(jnp.float32) * feat_ref[2].astype(jnp.float32)
+    ).astype(jnp.bfloat16)
+
+    def dot(x, y):
+        return jnp.dot(x, y, preferred_element_type=jnp.float32)
+
+    filt = filt_ref[...]
+    filt_hi = filt.astype(jnp.bfloat16)
+    filt_lo = (filt - filt_hi.astype(jnp.float32)).astype(jnp.bfloat16)
+    spec = (
+        dot(fwd_ref[0, :, :taps], filt_hi)
+        + dot(fwd_ref[1, :, :taps], filt_hi)
+        + dot(fwd_ref[0, :, :taps], filt_lo)
+    )
+    spec_r, spec_i = spec[:taps], spec[taps:]
+    win_iota = lax.broadcasted_iota(jnp.int32, (2 * taps, 1), 0)
+    out_iota = lax.broadcasted_iota(jnp.int32, (taps, 1), 0)
+    for block in range(row_count // taps):
+        r0 = block * taps
+        start = jnp.int32(0)
+        for doc in range(lens_ref.shape[0] - 1):
+            end = start + lens_ref[doc]
+            first, last = start - base, end - base
+
+            @pl.when((last > r0) & (first < r0 + taps) & (first < last))
+            def _(first=first):
+                window = ext_ref[r0 : r0 + 2 * taps, :]
+                window = jnp.where(win_iota + (r0 - taps) >= first, window, jnp.zeros_like(window))
+                wave = dot(fwd_ref[0], window) + dot(fwd_ref[1], window)
+                wave_r, wave_i = wave[:taps], wave[taps:]
+                prod = jnp.concatenate(
+                    (
+                        (wave_r * spec_r - wave_i * spec_i).astype(jnp.bfloat16),
+                        (wave_r * spec_i + wave_i * spec_r).astype(jnp.bfloat16),
+                    ),
+                    axis=0,
+                )
+                sums = dot(inv_ref[0], prod) + dot(inv_ref[1], prod)
+                sum_ref[...] = jnp.where(out_iota + r0 >= first, sums, sum_ref[...])
+
+            start = end
+        out_ref[r0 : r0 + taps, :] = (
+            feat_ref[0, r0 : r0 + taps, :].astype(jnp.float32) * sum_ref[...]
+        ).astype(out_ref.dtype)
+
+
+def split_two(matrix):
+    high = matrix.astype(jnp.bfloat16)
+    low = (matrix - high.astype(np.float64)).astype(jnp.bfloat16)
+    return np.stack((high, low))
 
 
 def hyena_fast(features, short_filter, medium_filter, skip_gain, lengths):
     row_count, _, cols = features.shape
     taps = medium_filter.shape[0]
-    subs = cols // 128
     span_index = lax.axis_index("seq")
-    gated = (features[:, 1].astype(jnp.float32) * features[:, 2].astype(jnp.float32)).astype(
-        jnp.bfloat16
-    )
-    carried = passed_along(gated[row_count - taps :], "seq", 1)
-    ext = jnp.concatenate((carried, gated), axis=0).reshape(row_count + taps, subs, 128)
-    query = features[:, 0].reshape(row_count, subs, 128)
-    filt = medium_filter.at[: short_filter.shape[0]].add(short_filter)
-    filt = filt.at[0].add(skip_gain).astype(jnp.bfloat16).reshape(taps, subs, 128)
+    streams = features.transpose(1, 0, 2)
+    tail = streams[:, row_count - taps :]
+    gated_tail = (tail[1].astype(jnp.float32) * tail[2].astype(jnp.float32)).astype(jnp.bfloat16)
+    carried = passed_along(gated_tail, "seq", 1)
+    head = jnp.concatenate((short_filter[:1] + skip_gain[None, :], short_filter[1:]), axis=0)
+    filt = medium_filter + jnp.pad(head, ((0, taps - head.shape[0]), (0, 0)))
+    angle = np.pi / (2 * taps) * np.outer(2 * np.arange(taps) + 1, np.arange(2 * taps))
+    fwd = split_two(np.concatenate((np.cos(angle), -np.sin(angle)), axis=0))
+    inv = split_two(
+        np.concatenate((np.cos(angle), -np.sin(angle)), axis=0).T[taps:] / taps
+    )
     scalars = jnp.concatenate((lengths, jnp.reshape(span_index * row_count, (1,)).astype(jnp.int32)))
-    vmem = pl.BlockSpec(memory_space=pltpu.VMEM)
-    out = pl.pallas_call(
+    width = math.gcd(cols, 512)
+    return pl.pallas_call(
         lambda *refs: hyena_kernel(row_count, taps, *refs),
-        out_shape=jax.ShapeDtypeStruct((row_count, subs, 128), jnp.bfloat16),
-        in_specs=[pl.BlockSpec(memory_space=pltpu.SMEM), vmem, vmem, vmem],
-        out_specs=vmem,
-        scratch_shapes=[pltpu.VMEM((row_count + taps, subs, 128), jnp.bfloat16)],
-        compiler_params=pltpu.CompilerParams(vmem_limit_bytes=24 * 2**20),
+        grid=(cols // width,),
+        out_shape=jax.ShapeDtypeStruct((row_count, cols), jnp.bfloat16),
+        in_specs=[
+            pl.BlockSpec(memory_space=pltpu.SMEM),
+            pl.BlockSpec((3, row_count, width), lambda i: (0, 0, i)),
+            pl.BlockSpec((taps, width), lambda i: (0, i)),
+            pl.BlockSpec((taps, width), lambda i: (0, i)),
+            pl.BlockSpec(fwd.shape, lambda i: (0, 0, 0)),
+            pl.BlockSpec(inv.shape, lambda i: (0, 0, 0)),
+        ],
+        out_specs=pl.BlockSpec((row_count, width), lambda i: (0, i)),
+        scratch_shapes=[
+            pltpu.VMEM((row_count + taps, width), jnp.bfloat16),
+            pltpu.VMEM((taps, width), jnp.float32),
+        ],
+        compiler_params=pltpu.CompilerParams(vmem_limit_bytes=32 * 2**20),
         cost_estimate=pl.CostEstimate(
-            flops=2 * taps * row_count * cols * 10, bytes_accessed=7 * 2**20, transcendentals=0
+            flops=2 * 9 * 2 * taps * taps * 3 * cols, bytes_accessed=8 * 2**20, transcendentals=0
         ),
         name="hyena",
-    )(scalars, ext, query, filt)
-    return out.reshape(row_count, cols)
+    )(scalars, streams, carried, filt, fwd, inv)
 
 
 def doc_start(pos, lens_ref):
@@ -397,7 +414,7 @@
             out_ref[r : r + step, :] = (total / (w0 + w1 + w2)).astype(jnp.bfloat16)
 
 
-def attention_fast(attn_query, attn_key, attn_value, lengths):
+def attention_fast(attn_query, attn_key, attn_value, lengths, hyena_out):
     rows, cols = attn_query.shape
     span_index = lax.axis_index("seq")
     scalars = jnp.concatenate((lengths, jnp.reshape(span_index, (1,)).astype(jnp.int32)))
@@ -409,15 +426,16 @@
     sent = []
     for c in range(CHUNKS):
         sl = slice(c * width, (c + 1) * width)
-        qc, kc, vc = attn_query[:, sl], attn_key[:, sl], attn_value[:, sl]
+        qc = attn_query[:, sl]
+        kv = jnp.concatenate((attn_key[:, sl], attn_value[:, sl]), axis=1)
         qa = lax.ppermute(qc, "seq", [(2, 1), (3, 2)])
         qb = lax.ppermute(qc, "seq", [(3, 1)])
-        kp = lax.ppermute(kc, "seq", [(0, 1)])
-        vp = lax.ppermute(vc, "seq", [(0, 1)])
-        sent.append((qa, qb, kp, vp))
+        sent.append((qa, qb, lax.ppermute(kv, "seq", [(0, 1)])))
+    scalars, hyena_out = lax.optimization_barrier((scalars, hyena_out))
+    other = pl.BlockSpec((rows, HD), lambda h: (0, heads + h))
     outs = []
     for c in range(CHUNKS):
-        qa, qb, kp, vp = sent[c]
+        qa, qb, kvp = sent[c]
         first = c * heads
         whole = pl.BlockSpec((rows, HD), lambda h, first=first: (0, first + h))
         own, lse, oa, ob = pl.pallas_call(
@@ -429,7 +447,7 @@
                 jax.ShapeDtypeStruct((rows + STAT_ROWS, width), jnp.bfloat16),
                 jax.ShapeDtypeStruct((rows + STAT_ROWS, width), jnp.bfloat16),
             ),
-            in_specs=[smem, whole, block, block, block, block, whole, whole],
+            in_specs=[smem, whole, block, block, block, other, whole, whole],
             out_specs=(block, block, tall, tall),
             scratch_shapes=[pltpu.VMEM((rows, rows), jnp.float32)] * 5,
             compiler_params=pltpu.CompilerParams(vmem_limit_bytes=32 * 2**20),
@@ -439,7 +457,7 @@
                 transcendentals=heads * 5 * rows * rows,
             ),
             name="attend",
-        )(scalars, attn_query, qa, qb, kp, vp, attn_key, attn_value)
+        )(scalars, attn_query, qa, qb, kvp, kvp, attn_key, attn_value)
         ra = lax.ppermute(oa, "seq", [(1, 2), (2, 3)])
         rb = lax.ppermute(ob, "seq", [(1, 3)])
         outs.append((own, lse, ra, rb))
@@ -458,7 +476,7 @@
                 name="merge",
             )(scalars, own, lse, ra, rb)
         )
-    return jnp.concatenate(merged, axis=1)
+    return hyena_out, jnp.concatenate(merged, axis=1)
 
 
 def local(
@@ -466,17 +484,15 @@
 ):
     rows, cols = attn_query.shape
     spans = lax.axis_size("seq")
-    if cols % 2048 == 0 and rows % 8 == 0:
+    taps = medium_filter.shape[0]
+    if cols % 128 == 0 and taps % 128 == 0 and rows % taps == 0:
         hyena = hyena_fast
     else:
         hyena = hyena_mix
+    hyena_out = hyena(features, short_filter, medium_filter, skip_gain, lengths)
     if spans == 4 and rows % 128 == 0 and rows <= 640 and cols % (CHUNKS * HD) == 0:
-        attention = attention_fast
-    else:
-        attention = attention_mix
-    hyena_out = hyena(features, short_filter, medium_filter, skip_gain, lengths)
-    attn_out = attention(attn_query, attn_key, attn_value, lengths)
-    return (hyena_out, attn_out)
+        return attention_fast(attn_query, attn_key, attn_value, lengths, hyena_out)
+    return (hyena_out, attention_mix(attn_query, attn_key, attn_value, lengths))
 
 
 def solution(mesh):

time: 192 us -> 162 us (0.84)
  starting transfers between devices: 44.1 us -> 18.3 us
  waiting for transfers between devices: 38.4 us -> 51.8 us
  Pallas kernels: 79.5 us -> 67.8 us
  local copies, waits for them, and re-layouts: 22.4 us -> 12.6 us
  other arithmetic: 5.1 us -> 9.37 us
    pallas_call x1, Pallas kernels: 39.9 us -> 13.5 us  [hyena_fast(): pl.pallas_call(lambda *refs: hyena_kernel(row_count, taps, *refs), grid=(...]
    pallas_call x4 -> x2, Pallas kernels: 25.1 us -> 42.2 us  [attention_fast(): pl.pallas_call(lambda *refs: attn_kernel(rows, *refs), grid=(heads,), out...]
    ppermute x4 -> x2, waiting for transfers between devices: 2.36 us -> 15.8 us  [attention_fast(): rb = lax.ppermute(ob, 'seq', [(1, 3)])]
    ppermute x4 -> x2, starting transfers between devices: 12.6 us -> 2.86 us  [attention_fast(): rb = lax.ppermute(ob, 'seq', [(1, 3)])]
    ppermute x4 -> x2, waiting for transfers between devices: 9.08 us -> 0.01 us  [attention_fast(): qa = lax.ppermute(qc, 'seq', [(2, 1), (3, 2)])]
    ppermute x8 -> x2, starting transfers between devices: 10.7 us -> 2.69 us  [attention_fast(): sent.append((qa, qb, lax.ppermute(kv, 'seq', [(0, 1)])))]
    unnamed x82 -> x38, local copies, waits for them, and re-layouts: 14.9 us -> 8.57 us
    ppermute x4 -> x2, starting transfers between devices: 8.23 us -> 2.66 us  [attention_fast(): ra = lax.ppermute(oa, 'seq', [(1, 2), (2, 3)])]
  transfers between devices with their start and end apart: 25 -> 11, of which waited for: 7 -> 6; matrix products, arithmetic and copies ran while one was open for 7% -> 5% of each run, Pallas kernels for 40% -> 38%
where the time goes in v2:
time: 162 us; the launch traced here: 161 us
  Pallas kernels  67.8 us (42%)
  waiting for transfers between devices  51.8 us (32%)
  starting transfers between devices  18.3 us (11%)
  local copies, waits for them, and re-layouts  12.6 us (8%)
  other arithmetic  9.37 us (6%)
    pallas_call x2, Pallas kernels, attention_fast(): pl.pallas_call(lambda *refs: attn_kernel(rows, *refs), grid=(heads,), out...  42.2 us
    ppermute x2, waiting for transfers between devices, attention_fast(): sent.append((qa, qb, lax.ppermute(kv, 'seq', [(0, 1)])))  22.6 us
    ppermute x2, waiting for transfers between devices, attention_fast(): rb = lax.ppermute(ob, 'seq', [(1, 3)])  15.8 us
    pallas_call x1, Pallas kernels, hyena_fast(): pl.pallas_call(lambda *refs: hyena_kernel(row_count, taps, *refs), grid=(...  13.5 us
    pallas_call x2, Pallas kernels, attention_fast(): pl.pallas_call(lambda *refs: merge_kernel(rows, *refs), grid=(heads,), ou...  12.1 us
    ppermute x2, waiting for transfers between devices, attention_fast(): ra = lax.ppermute(oa, 'seq', [(1, 2), (2, 3)])  9.76 us
    unnamed x38, local copies, waits for them, and re-layouts  8.57 us
    ppermute x1, starting transfers between devices, passed_along(): return lax.ppermute(value, axis, pairs)  4.79 us
  transfers between devices with their start and end apart: 11, of which 6 were waited for; matrix products, arithmetic and copies ran while one was open for 5% of the time, Pallas kernels for 38%

profile of v2, /device:TPU:10, one launch (start us, length us, event | category | flops | bytes accessed | tf_op | source)
XLA Modules:
  0.0 160.7 jit_solution(16745709088967069434)
XLA Ops:
  0.6 2.8 %fusion.4 = (bf16[384,1024]{1,0:T(8,128)(2,1)}, bf16[384,1024]{1,0:T(8,128)(2,1)}) fusion(bf16[384,2048]{1,0:T(8,128)(2,1)} %refs_1_.3), kind=kLoop, calls=%fused_computation.13 | loop fusion | bytes 3145728 | tf_op jit(solution)/shard_map/slice | solution.py:429
  3.4 1.4 collective-permute-start.6
  4.8 1.3 collective-permute-start.7
  6.1 2.1 %fusion.1 = bf16[128,2048]{1,0:T(8,128)(2,1)} fusion(bf16[3,384,2048]{2,1,0:T(8,128)(2,1)} %bitcast.6), kind=kLoop, calls=%fused_computation.7 | loop fusion | flops 1048576 | bytes 1572864 | tf_op jit(solution)/shard_map/convert_element_type | solution.py:235
  8.3 4.8 %collective-permute-start = (bf16[128,2048]{1,0:T(8,128)(2,1)}, bf16[128,2048]{1,0:T(8,128)(2,1)}, u32[]{:S(2)}, u32[]{:S(2)}) collective-permute-start(bf16[128,2048]{1,0:T(8,128)(2,1)} %fusion.1), channel_id=1, source_target_pairs={{0,4},{4,8},{8,12},{1,5},{5,9},{9,13},{2,6},{6,10},{10,14},{3,7},{... | collective-permute-start | bytes 1572872 | tf_op jit(solution)/shard_map/ppermute | solution.py:17
  17.3 1.4 collective-permute-start.3
  20.6 1.3 fusion.refs_3_
  22.0 3.3 %collective-permute-done.refs_2_ = bf16[128,2048]{1,0:T(8,128)(2,1)} collective-permute-done((bf16[128,2048]{1,0:T(8,128)(2,1)}, bf16[128,2048]{1,0:T(8,128)(2,1)}, u32[]{:S(2)}, u32[]{:S(2)}) %collective-permute-start) | collective-permute-done | bytes 524320 | tf_op jit(solution)/shard_map/ppermute | solution.py:17
  26.6 1.3 collective-permute-start.2
  27.9 2.3 %copy-done.7 = bf16[384,3,2048]{2,0,1:T(8,128)(2,1)S(1)} copy-done((bf16[384,3,2048]{2,0,1:T(8,128)(2,1)S(1)}, bf16[384,3,2048]{2,0,1:T(8,128)(2,1)}, u32[]{:S(2)}) %copy-start.7) | copy-done | bytes 4718616
  30.3 13.5 %hyena.1 = bf16[384,2048]{1,0:T(8,128)(2,1)} custom-call(s32[5]{0:T(128)S(1)} %get-tuple-element.28.refs_0_, bf16[3,384,2048]{2,1,0:T(8,128)(2,1)S(1)} %bitcast.7, bf16[128,2048]{1,0:T(8,128)(2,1)} %collective-permute-done.refs_2_, f32[128,2048]{1,0:T(8,128)S(1)} %fusion.refs_3_, bf16[2,256,256]{2,1,0:T(8,128)(2,1)S(1)} %copy-done.9, ...), custom_call_target="tpu_custom_call" | custom-call | flops 3623878656 | bytes 8388608 | tf_op jit(solution)/shard_map/hyena/pallas_call | solution.py:246
  44.1 14.9 %collective-permute-done.8.refs_4_.refs_5_ = bf16[384,2048]{1,0:T(8,128)(2,1)} collective-permute-done((bf16[384,2048]{1,0:T(8,128)(2,1)}, bf16[384,2048]{1,0:T(8,128)(2,1)}, u32[]{:S(2)}, u32[]{:S(2)}) %collective-permute-start.8) | collective-permute-done | bytes 1572896 | tf_op jit(solution)/shard_map/ppermute | solution.py:433
  59.0 20.8 %attend.3 = (f32[384,1024]{1,0:T(8,128)S(1)}, f32[384,1024]{1,0:T(8,128)S(1)}, bf16[400,1024]{1,0:T(8,128)(2,1)S(1)}, bf16[400,1024]{1,0:T(8,128)(2,1)S(1)}) custom-call(s32[5]{0:T(128)S(1)} %get-tuple-element.13.refs_0_, bf16[384,2048]{1,0:T(8,128)(2,1)S(1)} %copy-done, bf16[384,1024]{1,0:T(8,128)(2,1)} %collective-permute-done.6.refs_2_, ...), custom_call_target="tpu_custom_call" | custom-call | flops 6039797760 | bytes 8388608 | tf_op jit(solution)/shard_map/attend/pallas_call | solution.py:441
  80.9 1.3 collective-permute-start.9
  82.3 1.5 collective-permute-start.10
  83.8 7.7 %collective-permute-done.3.refs_4_.refs_5_ = bf16[384,2048]{1,0:T(8,128)(2,1)} collective-permute-done((bf16[384,2048]{1,0:T(8,128)(2,1)}, bf16[384,2048]{1,0:T(8,128)(2,1)}, u32[]{:S(2)}, u32[]{:S(2)}) %collective-permute-start.3) | collective-permute-done | bytes 1572896 | tf_op jit(solution)/shard_map/ppermute | solution.py:433
  91.6 21.4 %attend.2 = (f32[384,1024]{1,0:T(8,128)S(1)}, f32[384,1024]{1,0:T(8,128)S(1)}, bf16[400,1024]{1,0:T(8,128)(2,1)}, bf16[400,1024]{1,0:T(8,128)(2,1)}) custom-call(s32[5]{0:T(128)S(1)} %get-tuple-element.13.refs_0_, bf16[384,2048]{1,0:T(8,128)(2,1)S(1)} %copy-done, bf16[384,1024]{1,0:T(8,128)(2,1)S(1)} %collective-permute-done.1.refs_2_, ...), custom_call_target="tpu_custom_call" | custom-call | flops 6039797760 | bytes 8388608 | tf_op jit(solution)/shard_map/attend/pallas_call | solution.py:441
  115.3 1.3 collective-permute-start.4
  116.6 1.3 collective-permute-start.5
  119.8 6.0 %merge.3 = bf16[384,1024]{1,0:T(8,128)(2,1)} custom-call(s32[5]{0:T(128)} %copy-done.8, f32[384,1024]{1,0:T(8,128)} %copy-done.3, f32[384,1024]{1,0:T(8,128)} %copy-done.4, bf16[400,1024]{1,0:T(8,128)(2,1)} %copy-done.12, bf16[400,1024]{1,0:T(8,128)(2,1)} %copy-done.13), custom_call_target="tpu_custom_call" | custom-call | flops 6291456 | bytes 6291456 | tf_op jit(solution)/shard_map/merge/pallas_call | solution.py:467
  125.8 9.8 %collective-permute-done.4.refs_3_ = bf16[400,1024]{1,0:T(8,128)(2,1)S(1)} collective-permute-done((bf16[400,1024]{1,0:T(8,128)(2,1)}, bf16[400,1024]{1,0:T(8,128)(2,1)S(1)}, u32[]{:S(2)}, u32[]{:S(2)}) %collective-permute-start.4) | collective-permute-done | bytes 819232 | tf_op jit(solution)/shard_map/ppermute | solution.py:461
  135.6 15.8 %collective-permute-done.5.refs_4_ = bf16[400,1024]{1,0:T(8,128)(2,1)S(1)} collective-permute-done((bf16[400,1024]{1,0:T(8,128)(2,1)}, bf16[400,1024]{1,0:T(8,128)(2,1)S(1)}, u32[]{:S(2)}, u32[]{:S(2)}) %collective-permute-start.5) | collective-permute-done | bytes 819232 | tf_op jit(solution)/shard_map/ppermute | solution.py:462
  152.2 6.1 %merge.2 = bf16[384,1024]{1,0:T(8,128)(2,1)} custom-call(s32[5]{0:T(128)} %copy-done.8, f32[384,1024]{1,0:T(8,128)} %copy-done.5, f32[384,1024]{1,0:T(8,128)} %copy-done.6, bf16[400,1024]{1,0:T(8,128)(2,1)} %copy-done.14, bf16[400,1024]{1,0:T(8,128)(2,1)} %copy-done.15), custom_call_target="tpu_custom_call" | custom-call | flops 6291456 | bytes 6291456 | tf_op jit(solution)/shard_map/merge/pallas_call | solution.py:467
  158.3 2.4 %pad_maximum_fusion.2 = bf16[384,2048]{1,0:T(8,128)(2,1)} fusion(bf16[384,1024]{1,0:T(8,128)(2,1)S(1)} %copy-done.11, bf16[384,1024]{1,0:T(8,128)(2,1)} %merge.2), kind=kLoop, calls=%fused_computation.2 | loop fusion | flops 3145728 | bytes 3145728 | tf_op jit(solution)/shard_map/concatenate | solution.py:479
  (51 shorter events, 13.9 us)
Async XLA Ops:
  0.6 12.5 %copy-start.2 = (bf16[384,2048]{1,0:T(8,128)(2,1)S(1)}, bf16[384,2048]{1,0:T(8,128)(2,1)}, u32[]{:S(2)}) copy-start(bf16[384,2048]{1,0:T(8,128)(2,1)} %refs_7_.3) | copy-start | bytes 4718596
  3.4 9.7 %copy-start.1 = (bf16[384,2048]{1,0:T(8,128)(2,1)S(1)}, bf16[384,2048]{1,0:T(8,128)(2,1)}, u32[]{:S(2)}) copy-start(bf16[384,2048]{1,0:T(8,128)(2,1)} %refs_6_.3) | copy-start | bytes 4718596
  3.4 23.2 %collective-permute-start.6 = (bf16[384,1024]{1,0:T(8,128)(2,1)}, bf16[384,1024]{1,0:T(8,128)(2,1)}, u32[]{:S(2)}, u32[]{:S(2)}) collective-permute-start(bf16[384,1024]{1,0:T(8,128)(2,1)} %get-tuple-element.27), channel_id=1, source_target_pairs={{8,4},{12,8},{9,5},{13,9},{10,6},{14,10},{11,7},{15,11},{24,20},{2... | collective-permute-start | bytes 2359304 | tf_op jit(solution)/shard_map/ppermute | solution.py:431
  4.8 39.2 %collective-permute-start.7 = (bf16[384,1024]{1,0:T(8,128)(2,1)}, bf16[384,1024]{1,0:T(8,128)(2,1)}, u32[]{:S(2)}, u32[]{:S(2)}) collective-permute-start(bf16[384,1024]{1,0:T(8,128)(2,1)} %get-tuple-element.27), channel_id=1, source_target_pairs={{12,4},{13,5},{14,6},{15,7},{28,20},{29,21},{30,22},{31,23}} | collective-permute-start | bytes 2359304 | tf_op jit(solution)/shard_map/ppermute | solution.py:432
  8.3 17.0 %collective-permute-start = (bf16[128,2048]{1,0:T(8,128)(2,1)}, bf16[128,2048]{1,0:T(8,128)(2,1)}, u32[]{:S(2)}, u32[]{:S(2)}) collective-permute-start(bf16[128,2048]{1,0:T(8,128)(2,1)} %fusion.1), channel_id=1, source_target_pairs={{0,4},{4,8},{8,12},{1,5},{5,9},{9,13},{2,6},{6,10},{10,14},{3,7},{... | collective-permute-start | bytes 1572872 | tf_op jit(solution)/shard_map/ppermute | solution.py:17
  14.7 44.3 %collective-permute-start.8 = (bf16[384,2048]{1,0:T(8,128)(2,1)}, bf16[384,2048]{1,0:T(8,128)(2,1)}, u32[]{:S(2)}, u32[]{:S(2)}) collective-permute-start(bf16[384,2048]{1,0:T(8,128)(2,1)} %pad_maximum_fusion.1), channel_id=1, source_target_pairs={{0,4},{1,5},{2,6},{3,7},{16,20},{17,21},{18,22},{19,23}} | collective-permute-start | bytes 4718600 | tf_op jit(solution)/shard_map/ppermute | solution.py:433
  16.0 2.7 %copy-start.17 = (f32[2048]{0:T(1024)S(1)}, f32[2048]{0:T(1024)}, u32[]{:S(2)}) copy-start(f32[2048]{0:T(1024)} %param.13) | copy-start | bytes 24580
  16.0 3.6 %copy-start.18 = (s32[4]{0:T(128)S(1)}, s32[4]{0:T(128)}, u32[]{:S(2)}) copy-start(s32[4]{0:T(128)} %param.17) | copy-start | bytes 52
  17.3 10.6 %copy-start.9 = (bf16[2,256,256]{2,1,0:T(8,128)(2,1)S(1)}, bf16[2,256,256]{2,1,0:T(8,128)(2,1)}, u32[]{:S(2)}) copy-start(bf16[2,256,256]{2,1,0:T(8,128)(2,1)} %constant.14.clone.refs_4_) | copy-start | bytes 786436
  17.3 10.6 %copy-start.10 = (bf16[2,128,256]{2,1,0:T(8,128)(2,1)S(1)}, bf16[2,128,256]{2,1,0:T(8,128)(2,1)}, u32[]{:S(2)}) copy-start(bf16[2,128,256]{2,1,0:T(8,128)(2,1)} %constant.15.clone.refs_5_) | copy-start | bytes 393220
  17.3 74.2 %collective-permute-start.3 = (bf16[384,2048]{1,0:T(8,128)(2,1)}, bf16[384,2048]{1,0:T(8,128)(2,1)}, u32[]{:S(2)}, u32[]{:S(2)}) collective-permute-start(bf16[384,2048]{1,0:T(8,128)(2,1)} %pad_maximum_fusion), channel_id=1, source_target_pairs={{0,4},{1,5},{2,6},{3,7},{16,20},{17,21},{18,22},{19,23}} | collective-permute-start | bytes 4718600 | tf_op jit(solution)/shard_map/ppermute | solution.py:433
  19.6 5.7 %copy-start.16 = (bf16[384,1024]{1,0:T(8,128)(2,1)S(1)}, bf16[384,1024]{1,0:T(8,128)(2,1)}, u32[]{:S(2)}) copy-start(bf16[384,1024]{1,0:T(8,128)(2,1)} %get-tuple-element.26) | copy-start | bytes 2359300
  19.7 71.8 %copy-start.8 = (s32[5]{0:T(128)}, s32[5]{0:T(128)S(1)}, u32[]{:S(2)}) copy-start(s32[5]{0:T(128)S(1)} %get-tuple-element.13.refs_0_) | copy-start | bytes 64
  25.3 58.5 %collective-permute-start.1 = (bf16[384,1024]{1,0:T(8,128)(2,1)S(1)}, bf16[384,1024]{1,0:T(8,128)(2,1)S(1)}, u32[]{:S(2)}, u32[]{:S(2)}) collective-permute-start(bf16[384,1024]{1,0:T(8,128)(2,1)S(1)} %copy-done.16), channel_id=1, source_target_pairs={{8,4},{12,8},{9,5},{13,9},{10,6},{14,10},{11,7},{15,11},{24,20},{2... | collective-permute-start | bytes 2359304 | tf_op jit(solution)/shard_map/ppermute | solution.py:431
  26.6 57.2 %collective-permute-start.2 = (bf16[384,1024]{1,0:T(8,128)(2,1)S(1)}, bf16[384,1024]{1,0:T(8,128)(2,1)S(1)}, u32[]{:S(2)}, u32[]{:S(2)}) collective-permute-start(bf16[384,1024]{1,0:T(8,128)(2,1)S(1)} %copy-done.16), channel_id=1, source_target_pairs={{12,4},{13,5},{14,6},{15,7},{28,20},{29,21},{30,22},{31,23}} | collective-permute-start | bytes 2359304 | tf_op jit(solution)/shard_map/ppermute | solution.py:432
  27.9 2.3 %copy-start.7 = (bf16[384,3,2048]{2,0,1:T(8,128)(2,1)S(1)}, bf16[384,3,2048]{2,0,1:T(8,128)(2,1)}, u32[]{:S(2)}) copy-start(bf16[384,3,2048]{2,0,1:T(8,128)(2,1)} %param.10) | copy-start | bytes 14155780
  30.3 28.7 %copy-start = (bf16[384,2048]{1,0:T(8,128)(2,1)S(1)}, bf16[384,2048]{1,0:T(8,128)(2,1)}, u32[]{:S(2)}) copy-start(bf16[384,2048]{1,0:T(8,128)(2,1)} %refs_1_.3) | copy-start | bytes 4718596
  80.9 32.0 %copy-start.3 = (f32[384,1024]{1,0:T(8,128)}, f32[384,1024]{1,0:T(8,128)S(1)}, u32[]{:S(2)}) copy-start(f32[384,1024]{1,0:T(8,128)S(1)} %get-tuple-element.18.refs_1_) | copy-start | bytes 4718596
  80.9 37.0 %collective-permute-start.9 = (bf16[400,1024]{1,0:T(8,128)(2,1)S(1)}, bf16[400,1024]{1,0:T(8,128)(2,1)S(1)}, u32[]{:S(2)}, u32[]{:S(2)}) collective-permute-start(bf16[400,1024]{1,0:T(8,128)(2,1)S(1)} %get-tuple-element.20), channel_id=1, source_target_pairs={{4,8},{8,12},{5,9},{9,13},{6,10},{10,14},{7,11},{11,15},{20,24},{2... | collective-permute-start | bytes 2457608 | tf_op jit(solution)/shard_map/ppermute | solution.py:461
  82.3 35.7 %collective-permute-start.10 = (bf16[400,1024]{1,0:T(8,128)(2,1)S(1)}, bf16[400,1024]{1,0:T(8,128)(2,1)S(1)}, u32[]{:S(2)}, u32[]{:S(2)}) collective-permute-start(bf16[400,1024]{1,0:T(8,128)(2,1)S(1)} %get-tuple-element.21), channel_id=1, source_target_pairs={{4,12},{5,13},{6,14},{7,15},{20,28},{21,29},{22,30},{23,31}} | collective-permute-start | bytes 2457608 | tf_op jit(solution)/shard_map/ppermute | solution.py:462
  115.3 20.3 %collective-permute-start.4 = (bf16[400,1024]{1,0:T(8,128)(2,1)}, bf16[400,1024]{1,0:T(8,128)(2,1)S(1)}, u32[]{:S(2)}, u32[]{:S(2)}) collective-permute-start(bf16[400,1024]{1,0:T(8,128)(2,1)} %get-tuple-element.16), channel_id=1, source_target_pairs={{4,8},{8,12},{5,9},{9,13},{6,10},{10,14},{7,11},{11,15},{20,24},{2... | collective-permute-start | bytes 2457608 | tf_op jit(solution)/shard_map/ppermute | solution.py:461
  116.6 34.7 %collective-permute-start.5 = (bf16[400,1024]{1,0:T(8,128)(2,1)}, bf16[400,1024]{1,0:T(8,128)(2,1)S(1)}, u32[]{:S(2)}, u32[]{:S(2)}) collective-permute-start(bf16[400,1024]{1,0:T(8,128)(2,1)} %get-tuple-element.17), channel_id=1, source_target_pairs={{4,12},{5,13},{6,14},{7,15},{20,28},{21,29},{22,30},{23,31}} | collective-permute-start | bytes 2457608 | tf_op jit(solution)/shard_map/ppermute | solution.py:462
  135.6 15.8 %copy-start.14 = (bf16[400,1024]{1,0:T(8,128)(2,1)}, bf16[400,1024]{1,0:T(8,128)(2,1)S(1)}, u32[]{:S(2)}) copy-start(bf16[400,1024]{1,0:T(8,128)(2,1)S(1)} %collective-permute-done.4.refs_3_) | copy-start | bytes 2457604
  152.2 6.1 %copy-start.11 = (bf16[384,1024]{1,0:T(8,128)(2,1)S(1)}, bf16[384,1024]{1,0:T(8,128)(2,1)}, u32[]{:S(2)}) copy-start(bf16[384,1024]{1,0:T(8,128)(2,1)} %merge.3) | copy-start | bytes 2359300
  (6 other events, 6.2 us)

commit v3 on v2

--- a/solution.py
+++ b/solution.py
@@ -165,7 +165,6 @@
 LN2 = 0.6931471805599453
 SCALE2 = HD**-0.5 * LOG2E
 NEG = -1e30
-CHUNKS = 2
 STAT_ROWS = 16
 
 
@@ -277,32 +276,91 @@
     return start
 
 
+def attend(query_ref, keys, values, biases, emit):
+    rows = query_ref.shape[0]
+    step = 128
+    ones = jnp.ones((rows, 128), jnp.bfloat16)
+    vals = [jnp.concatenate((v[...], ones), axis=1) for v in values]
+    for r in range(0, rows, step):
+        q = query_ref[r : r + step, :]
+        scores = [
+            lax.dot_general(q, k[...], (((1,), (1,)), ((), ())),
+                            preferred_element_type=jnp.float32) + b[r : r + step, :]
+            for k, b in zip(keys, biases)
+        ]
+        top = jnp.max(scores[0], axis=1, keepdims=True)
+        for s in scores[1:]:
+            top = jnp.maximum(top, jnp.max(s, axis=1, keepdims=True))
+        acc = None
+        for s, v in zip(scores, vals):
+            w = jnp.exp2((s - top) * SCALE2).astype(jnp.bfloat16)
+            part = jnp.dot(w, v, preferred_element_type=jnp.float32)
+            acc = part if acc is None else acc + part
+        total = acc[:, 128:]
+        emit(r, acc[:, :128] / total, top * SCALE2 + jnp.log2(total))
+
+
+def needs(lens_ref, base, rows, ahead, back):
+    q_first = base + ahead * rows
+    start = jnp.int32(0)
+    end = jnp.int32(0)
+    for doc in range(lens_ref.shape[0] - 1):
+        end = end + lens_ref[doc]
+        start = jnp.where(q_first >= end, end, start)
+    return start < base + (1 - back) * rows
+
+
+def fill_bias(lens_ref, base, rows, ref, ahead, back):
+    qpos = base + ahead * rows + lax.broadcasted_iota(jnp.int32, (rows, 1), 0)
+    starts = doc_start(qpos, lens_ref)
+    kpos = base - back * rows + lax.broadcasted_iota(jnp.int32, (1, rows), 1)
+    ref[...] = jnp.where((kpos <= qpos) & (kpos >= starts), 0.0, NEG).astype(jnp.float32)
+
+
+def near_kernel(rows, lens_ref, q_ref, k_ref, v_ref, k1_ref, v1_ref, k2_ref, v2_ref, all_ref, o_ref,
+                b0, b1, b2):
+    span = lens_ref[lens_ref.shape[0] - 1]
+    base = span * rows
+    one = (span >= 1) & needs(lens_ref, base, rows, 0, 1)
+    two = (span >= 2) & needs(lens_ref, base, rows, 0, 2)
+
+    @pl.when(pl.program_id(0) == 0)
+    def _():
+        fill_bias(lens_ref, base, rows, b0, 0, 0)
+        pl.when(one)(lambda: fill_bias(lens_ref, base, rows, b1, 0, 1))
+        pl.when(two)(lambda: fill_bias(lens_ref, base, rows, b2, 0, 2))
+
+    def emit(r, out, lse):
+        o_ref[r : r + 128, :] = out.astype(jnp.bfloat16)
+
+    pl.when(two)(
+        lambda: attend(q_ref, (k_ref, k1_ref, k2_ref), (v_ref, v1_ref, v2_ref), (b0, b1, b2), emit)
+    )
+    pl.when(one & jnp.logical_not(two))(
+        lambda: attend(q_ref, (k_ref, k1_ref), (v_ref, v1_ref), (b0, b1), emit)
+    )
+    pl.when(jnp.logical_not(one))(lambda: attend(q_ref, (k_ref,), (v_ref,), (b0,), emit))
+
+
 def attn_kernel(rows, lens_ref, q_ref, qa_ref, qb_ref, kp_ref, vp_ref, k_ref, v_ref,
                 o_ref, lse_ref, oa_ref, ob_ref, b00, b10, b01, b11, b02):
     span = lens_ref[lens_ref.shape[0] - 1]
     base = span * rows
 
-    def needs(ahead, back):
-        q_first = base + ahead * rows
-        start = jnp.int32(0)
-        end = jnp.int32(0)
-        for doc in range(lens_ref.shape[0] - 1):
-            end = end + lens_ref[doc]
-            start = jnp.where(q_first >= end, end, start)
-        return start < base + (1 - back) * rows
-
-    own_prev = (span == 1) & needs(0, 1)
-    a_here = ((span == 1) | (span == 2)) & needs(1, 0)
-    a_prev = (span == 1) & needs(1, 1)
-    b_here = (span == 1) & needs(2, 0)
+    def reads(ahead, back):
+        return needs(lens_ref, base, rows, ahead, back)
+
+    own_prev = (span == 1) & reads(0, 1)
+    a_here = ((span == 1) | (span == 2)) & reads(1, 0)
+    a_prev = (span == 1) & reads(1, 1)
+    b_here = (span == 1) & reads(2, 0)
 
     @pl.when(pl.program_id(0) == 0)
     def _():
+        lse_ref[...] = jnp.zeros_like(lse_ref)
+
         def fill(ref, ahead, back):
-            qpos = base + ahead * rows + lax.broadcasted_iota(jnp.int32, (rows, 1), 0)
-            starts = doc_start(qpos, lens_ref)
-            kpos = base - back * rows + lax.broadcasted_iota(jnp.int32, (1, rows), 1)
-            ref[...] = jnp.where((kpos <= qpos) & (kpos >= starts), 0.0, NEG).astype(jnp.float32)
+            fill_bias(lens_ref, base, rows, ref, ahead, back)
 
         fill(b00, 0, 0)
         pl.when(own_prev)(lambda: fill(b01, 0, 1))
@@ -311,31 +369,11 @@
         pl.when(b_here)(lambda: fill(b02, 2, 0))
 
     step = 128
-    ones = jnp.ones((rows, 128), jnp.bfloat16)
-
-    def attend(query_ref, keys, values, biases, emit):
-        vals = [jnp.concatenate((v[...], ones), axis=1) for v in values]
-        for r in range(0, rows, step):
-            q = query_ref[r : r + step, :]
-            scores = [
-                lax.dot_general(q, k[...], (((1,), (1,)), ((), ())),
-                                preferred_element_type=jnp.float32) + b[r : r + step, :]
-                for k, b in zip(keys, biases)
-            ]
-            top = jnp.max(scores[0], axis=1, keepdims=True)
-            for s in scores[1:]:
-                top = jnp.maximum(top, jnp.max(s, axis=1, keepdims=True))
-            acc = None
-            for s, v in zip(scores, vals):
-                w = jnp.exp2((s - top) * SCALE2).astype(jnp.bfloat16)
-                part = jnp.dot(w, v, preferred_element_type=jnp.float32)
-                acc = part if acc is None else acc + part
-            total = acc[:, 128:]
-            emit(r, acc[:, :128] / total, top * SCALE2 + jnp.log2(total))
+    head_lane = lax.broadcasted_iota(jnp.int32, (step, 128), 1) == pl.program_id(0)
 
     def emit_own(r, out, lse):
-        o_ref[r : r + step, :] = out
-        lse_ref[r : r + step, :] = lse
+        o_ref[r : r + step, :] = out.astype(jnp.bfloat16)
+        lse_ref[r : r + step, :] = jnp.where(head_lane, lse, lse_ref[r : r + step, :])
 
     eye = lax.broadcasted_iota(jnp.int32, (128, 128), 0) == lax.broadcasted_iota(
         jnp.int32, (128, 128), 1
@@ -374,7 +412,7 @@
     pl.when(jnp.logical_not(b_here))(lambda: empty(ob_ref))
 
 
-def merge_kernel(rows, lens_ref, o_ref, lse_ref, ra_ref, rb_ref, out_ref):
+def merge_kernel(rows, lens_ref, o_ref, lse_ref, ra_ref, rb_ref, all_ref, out_ref):
     span = lens_ref[lens_ref.shape[0] - 1]
     step = 128
     eye = lax.broadcasted_iota(jnp.int32, (128, 128), 0) == lax.broadcasted_iota(
@@ -383,11 +421,12 @@
 
     @pl.when(span < 2)
     def _():
-        out_ref[...] = o_ref[...].astype(jnp.bfloat16)
+        out_ref[...] = o_ref[...]
 
     @pl.when(span >= 2)
     def _():
         blocks = rows // step
+        head_lane = lax.broadcasted_iota(jnp.int32, (step, 128), 1) == pl.program_id(0)
         stat_a = ra_ref[rows:, :].astype(jnp.float32)
         stat_b = rb_ref[rows:, :].astype(jnp.float32)
 
@@ -399,7 +438,7 @@
 
         for i in range(blocks):
             r = i * step
-            own = lse_ref[r : r + step, :]
+            own = jnp.sum(jnp.where(head_lane, lse_ref[r : r + step, :], 0.0), axis=1, keepdims=True)
             lse_a = column(stat_a, i)
             lse_b = jnp.where(span == 3, column(stat_b, i), NEG)
             top = jnp.maximum(own, jnp.maximum(lse_a, lse_b))
@@ -407,7 +446,7 @@
             w1 = jnp.exp2(lse_a - top)
             w2 = jnp.exp2(lse_b - top)
             total = (
-                o_ref[r : r + step, :] * w0
+                o_ref[r : r + step, :].astype(jnp.float32) * w0
                 + ra_ref[r : r + step, :].astype(jnp.float32) * w1
                 + rb_ref[r : r + step, :].astype(jnp.float32) * w2
             )
@@ -418,37 +457,47 @@
     rows, cols = attn_query.shape
     span_index = lax.axis_index("seq")
     scalars = jnp.concatenate((lengths, jnp.reshape(span_index, (1,)).astype(jnp.int32)))
-    width = cols // CHUNKS
-    heads = width // HD
+    all_heads = cols // HD
+    heads = all_heads * 3 // 8
+    near = all_heads - 2 * heads
+    width = heads * HD
     smem = pl.BlockSpec(memory_space=pltpu.SMEM)
     block = pl.BlockSpec((rows, HD), lambda h: (0, h))
     tall = pl.BlockSpec((rows + STAT_ROWS, HD), lambda h: (0, h))
+    packed = pl.BlockSpec((rows, 128), lambda h: (0, 0))
+
+    def at(offset):
+        return pl.BlockSpec((rows, HD), lambda h: (0, offset + h))
+
+    def pair(lo, hi):
+        return jnp.concatenate((attn_key[:, lo:hi], attn_value[:, lo:hi]), axis=1)
+
     sent = []
-    for c in range(CHUNKS):
-        sl = slice(c * width, (c + 1) * width)
-        qc = attn_query[:, sl]
-        kv = jnp.concatenate((attn_key[:, sl], attn_value[:, sl]), axis=1)
+    for c in range(2):
+        qc = attn_query[:, c * width : (c + 1) * width]
         qa = lax.ppermute(qc, "seq", [(2, 1), (3, 2)])
         qb = lax.ppermute(qc, "seq", [(3, 1)])
+        kv = pair(c * width, (c + 1) * width)
         sent.append((qa, qb, lax.ppermute(kv, "seq", [(0, 1)])))
+    kv = pair(2 * width, cols)
+    kv1 = lax.ppermute(kv, "seq", [(0, 1), (1, 2), (2, 3)])
+    kv2 = lax.ppermute(kv, "seq", [(0, 2), (1, 3)])
     scalars, hyena_out = lax.optimization_barrier((scalars, hyena_out))
-    other = pl.BlockSpec((rows, HD), lambda h: (0, heads + h))
     outs = []
-    for c in range(CHUNKS):
+    for c in range(2):
         qa, qb, kvp = sent[c]
-        first = c * heads
-        whole = pl.BlockSpec((rows, HD), lambda h, first=first: (0, first + h))
+        whole = at(c * heads)
         own, lse, oa, ob = pl.pallas_call(
             lambda *refs: attn_kernel(rows, *refs),
             grid=(heads,),
             out_shape=(
-                jax.ShapeDtypeStruct((rows, width), jnp.float32),
-                jax.ShapeDtypeStruct((rows, width), jnp.float32),
+                jax.ShapeDtypeStruct((rows, width), jnp.bfloat16),
+                jax.ShapeDtypeStruct((rows, 128), jnp.float32),
                 jax.ShapeDtypeStruct((rows + STAT_ROWS, width), jnp.bfloat16),
                 jax.ShapeDtypeStruct((rows + STAT_ROWS, width), jnp.bfloat16),
             ),
-            in_specs=[smem, whole, block, block, block, other, whole, whole],
-            out_specs=(block, block, tall, tall),
+            in_specs=[smem, whole, block, block, block, at(heads), whole, whole],
+            out_specs=(block, packed, tall, tall),
             scratch_shapes=[pltpu.VMEM((rows, rows), jnp.float32)] * 5,
             compiler_params=pltpu.CompilerParams(vmem_limit_bytes=32 * 2**20),
             cost_estimate=pl.CostEstimate(
@@ -461,22 +510,40 @@
         ra = lax.ppermute(oa, "seq", [(1, 2), (2, 3)])
         rb = lax.ppermute(ob, "seq", [(1, 3)])
         outs.append((own, lse, ra, rb))
-    merged = []
-    for own, lse, ra, rb in outs:
-        merged.append(
-            pl.pallas_call(
-                lambda *refs: merge_kernel(rows, *refs),
-                grid=(heads,),
-                out_shape=jax.ShapeDtypeStruct((rows, width), jnp.bfloat16),
-                in_specs=[smem, block, block, tall, tall],
-                out_specs=block,
-                cost_estimate=pl.CostEstimate(
-                    flops=rows * width * 16, bytes_accessed=6 * 2**20, transcendentals=0
-                ),
-                name="merge",
-            )(scalars, own, lse, ra, rb)
-        )
-    return hyena_out, jnp.concatenate(merged, axis=1)
+        scalars, _ = lax.optimization_barrier((scalars, own))
+    anywhere = pl.BlockSpec(memory_space=pl.ANY)
+    whole_out = jax.ShapeDtypeStruct((rows, cols), jnp.bfloat16)
+    mine = at(2 * heads)
+    result = pl.pallas_call(
+        lambda *refs: near_kernel(rows, *refs[:8], None, *refs[8:]),
+        grid=(near,),
+        out_shape=whole_out,
+        in_specs=[smem, mine, mine, mine, block, at(near), block, at(near)],
+        out_specs=mine,
+        scratch_shapes=[pltpu.VMEM((rows, rows), jnp.float32)] * 3,
+        compiler_params=pltpu.CompilerParams(vmem_limit_bytes=32 * 2**20),
+        cost_estimate=pl.CostEstimate(
+            flops=near * 3 * rows * rows * HD * 4 * 2,
+            bytes_accessed=4 * 2**20,
+            transcendentals=near * 3 * rows * rows,
+        ),
+        name="near",
+    )(scalars, attn_query, attn_key, attn_value, kv1, kv1, kv2, kv2)
+    for c in range(2):
+        own, lse, ra, rb = outs[c]
+        result = pl.pallas_call(
+            lambda *refs: merge_kernel(rows, *refs),
+            grid=(heads,),
+            out_shape=whole_out,
+            in_specs=[smem, block, packed, tall, tall, anywhere],
+            out_specs=at(c * heads),
+            input_output_aliases={5: 0},
+            cost_estimate=pl.CostEstimate(
+                flops=rows * width * 16, bytes_accessed=4 * 2**20, transcendentals=0
+            ),
+            name="merge",
+        )(scalars, own, lse, ra, rb, result)
+    return hyena_out, result
 
 
 def local(
@@ -490,7 +557,7 @@
     else:
         hyena = hyena_mix
     hyena_out = hyena(features, short_filter, medium_filter, skip_gain, lengths)
-    if spans == 4 and rows % 128 == 0 and rows <= 640 and cols % (CHUNKS * HD) == 0:
+    if spans == 4 and rows % 128 == 0 and rows <= 640 and cols % (8 * HD) == 0:
         return attention_fast(attn_query, attn_key, attn_value, lengths, hyena_out)
     return (hyena_out, attention_mix(attn_query, attn_key, attn_value, lengths))
 

time: 162 us -> 156 us (0.963)
  Pallas kernels: 67.8 us -> 62.9 us
  starting transfers between devices: 18.3 us -> 22.9 us
  local copies, waits for them, and re-layouts: 12.6 us -> 8.21 us
  other arithmetic: 9.37 us -> 6.64 us
    ppermute x2, waiting for transfers between devices: 22.6 us -> 6.44 us  [attention_fast(): sent.append((qa, qb, lax.ppermute(kv, 'seq', [(0, 1)])))]
    pallas_call x2, Pallas kernels: 42.2 us -> 32 us  [attention_fast(): pl.pallas_call(lambda *refs: attn_kernel(rows, *refs), grid=(heads,), out...]
    ppermute x2, waiting for transfers between devices: 9.76 us -> 18.4 us  [attention_fast(): ra = lax.ppermute(oa, 'seq', [(1, 2), (2, 3)])]
    ppermute x2, waiting for transfers between devices: 15.8 us -> 23.4 us  [attention_fast(): rb = lax.ppermute(ob, 'seq', [(1, 3)])]
    pallas_call x0 -> x1, Pallas kernels: none -> 5.89 us  [attention_fast(): pl.pallas_call(lambda *refs: near_kernel(rows, *refs[:8], None, *refs[8:]...]
    unnamed x38 -> x36, local copies, waits for them, and re-layouts: 8.57 us -> 4.76 us
    ppermute x0 -> x2, starting transfers between devices: none -> 3.24 us  [the longest x1 1.91 us: attention_fast(): kv1 = lax.ppermute(kv, 'seq', [(0, 1), (1, 2), (2, 3)])]
    pallas_call x2, Pallas kernels: 12.1 us -> 9.26 us  [attention_fast(): pl.pallas_call(lambda *refs: merge_kernel(rows, *refs), grid=(heads,), ou...]
  transfers between devices with their start and end apart: 11 -> 13, of which waited for: 6 -> 7; matrix products, arithmetic and copies ran while one was open for 5% -> 5% of each run, Pallas kernels for 38% -> 38%
where the time goes in v3:
time: 156 us; the launch traced here: 154 us
  Pallas kernels  62.9 us (40%)
  waiting for transfers between devices  52.2 us (33%)
  starting transfers between devices  22.9 us (15%)
  local copies, waits for them, and re-layouts  8.21 us (5%)
  other arithmetic  6.64 us (4%)
    pallas_call x2, Pallas kernels, attention_fast(): pl.pallas_call(lambda *refs: attn_kernel(rows, *refs), grid=(heads,), out...  32 us
    ppermute x2, waiting for transfers between devices, attention_fast(): rb = lax.ppermute(ob, 'seq', [(1, 3)])  23.4 us
    ppermute x2, waiting for transfers between devices, attention_fast(): ra = lax.ppermute(oa, 'seq', [(1, 2), (2, 3)])  18.4 us
    pallas_call x1, Pallas kernels, hyena_fast(): pl.pallas_call(lambda *refs: hyena_kernel(row_count, taps, *refs), grid=(...  15.8 us
    pallas_call x2, Pallas kernels, attention_fast(): pl.pallas_call(lambda *refs: merge_kernel(rows, *refs), grid=(heads,), ou...  9.26 us
    ppermute x2, waiting for transfers between devices, attention_fast(): sent.append((qa, qb, lax.ppermute(kv, 'seq', [(0, 1)])))  6.44 us
    pallas_call x1, Pallas kernels, attention_fast(): pl.pallas_call(lambda *refs: near_kernel(rows, *refs[:8], None, *refs[8:]...  5.89 us
    unnamed x36, local copies, waits for them, and re-layouts  4.76 us
  transfers between devices with their start and end apart: 13, of which 7 were waited for; matrix products, arithmetic and copies ran while one was open for 5% of the time, Pallas kernels for 38%

profile of v3, /device:TPU:10, one launch (start us, length us, event | category | flops | bytes accessed | tf_op | source)
XLA Modules:
  0.0 153.7 jit_solution(15707749023625862258)
XLA Ops:
  0.7 2.5 %fusion.4 = (bf16[384,768]{1,0:T(8,128)(2,1)}, bf16[384,768]{1,0:T(8,128)(2,1)}) fusion(bf16[384,2048]{1,0:T(8,128)(2,1)} %refs_1_.5), kind=kLoop, calls=%fused_computation.13 | loop fusion | bytes 2359296 | tf_op jit(solution)/shard_map/slice | solution.py:477
  5.7 2.1 %fusion.1 = bf16[128,2048]{1,0:T(8,128)(2,1)} fusion(bf16[3,384,2048]{2,1,0:T(8,128)(2,1)} %bitcast.6), kind=kLoop, calls=%fused_computation.7 | loop fusion | flops 1048576 | bytes 1572864 | tf_op jit(solution)/shard_map/convert_element_type | solution.py:234
  7.9 4.7 %collective-permute-start = (bf16[128,2048]{1,0:T(8,128)(2,1)}, bf16[128,2048]{1,0:T(8,128)(2,1)}, u32[]{:S(2)}, u32[]{:S(2)}) collective-permute-start(bf16[128,2048]{1,0:T(8,128)(2,1)} %fusion.1), channel_id=1, source_target_pairs={{0,4},{4,8},{8,12},{1,5},{5,9},{9,13},{2,6},{6,10},{10,14},{3,7},{... | collective-permute-start | bytes 1572872 | tf_op jit(solution)/shard_map/ppermute | solution.py:17
  13.9 1.4 collective-permute-start.3
  20.9 4.0 %collective-permute-done.refs_2_ = bf16[128,2048]{1,0:T(8,128)(2,1)} collective-permute-done((bf16[128,2048]{1,0:T(8,128)(2,1)}, bf16[128,2048]{1,0:T(8,128)(2,1)}, u32[]{:S(2)}, u32[]{:S(2)}) %collective-permute-start) | collective-permute-done | bytes 524320 | tf_op jit(solution)/shard_map/ppermute | solution.py:17
  27.5 2.3 %copy-done.6 = bf16[384,3,2048]{2,0,1:T(8,128)(2,1)S(1)} copy-done((bf16[384,3,2048]{2,0,1:T(8,128)(2,1)S(1)}, bf16[384,3,2048]{2,0,1:T(8,128)(2,1)}, u32[]{:S(2)}) %copy-start.6) | copy-done | bytes 4718616
  29.8 15.8 %hyena.1 = bf16[384,2048]{1,0:T(8,128)(2,1)} custom-call(s32[5]{0:T(128)S(1)} %get-tuple-element.32.refs_0_, bf16[3,384,2048]{2,1,0:T(8,128)(2,1)S(1)} %bitcast.7, bf16[128,2048]{1,0:T(8,128)(2,1)} %collective-permute-done.refs_2_, f32[128,2048]{1,0:T(8,128)S(1)} %copy-done.3, bf16[2,256,256]{2,1,0:T(8,128)(2,1)S(1)} %copy-done.10, ...), custom_call_target="tpu_custom_call" | custom-call | flops 3623878656 | bytes 8388608 | tf_op jit(solution)/shard_map/hyena/pallas_call | solution.py:245
  45.6 1.9 %collective-permute-start.11 = (bf16[384,1024]{1,0:T(8,128)(2,1)S(1)}, bf16[384,1024]{1,0:T(8,128)(2,1)S(1)}, u32[]{:S(2)}, u32[]{:S(2)}) collective-permute-start(bf16[384,1024]{1,0:T(8,128)(2,1)S(1)} %pad_maximum_fusion.2), channel_id=1, source_target_pairs={{0,4},{4,8},{8,12},{1,5},{5,9},{9,13},{2,6},{6,10},{10,14},{3,7},{... | collective-permute-start | bytes 2359304 | tf_op jit(solution)/shard_map/ppermute | solution.py:483
  47.5 2.6 %collective-permute-done.3.refs_4_.refs_5_ = bf16[384,1536]{1,0:T(8,128)(2,1)} collective-permute-done((bf16[384,1536]{1,0:T(8,128)(2,1)}, bf16[384,1536]{1,0:T(8,128)(2,1)}, u32[]{:S(2)}, u32[]{:S(2)}) %collective-permute-start.3) | collective-permute-done | bytes 1179680 | tf_op jit(solution)/shard_map/ppermute | solution.py:481
  50.1 1.3 collective-permute-start.12
  51.5 15.7 %attend.2 = (bf16[384,768]{1,0:T(8,128)(2,1)S(1)}, f32[384,128]{1,0:T(8,128)S(1)}, bf16[400,768]{1,0:T(8,128)(2,1)S(1)}, bf16[400,768]{1,0:T(8,128)(2,1)S(1)}) custom-call(s32[5]{0:T(128)S(1)} %get-tuple-element.19.refs_0_, bf16[384,2048]{1,0:T(8,128)(2,1)S(1)} %copy-done.2, bf16[384,768]{1,0:T(8,128)(2,1)} %collective-permute-done.1.refs_2_, ...), custom_call_target="tpu_custom_call" | custom-call | flops 4529848320 | bytes 8388608 | tf_op jit(solution)/shard_map/attend/pallas_call | solution.py:490
  68.8 1.3 collective-permute-start.9
  70.1 1.5 collective-permute-start.10
  71.6 3.8 %collective-permute-done.6.refs_4_.refs_5_ = bf16[384,1536]{1,0:T(8,128)(2,1)} collective-permute-done((bf16[384,1536]{1,0:T(8,128)(2,1)}, bf16[384,1536]{1,0:T(8,128)(2,1)}, u32[]{:S(2)}, u32[]{:S(2)}) %collective-permute-start.6) | collective-permute-done | bytes 1179680 | tf_op jit(solution)/shard_map/ppermute | solution.py:481
  75.4 16.3 %attend.3 = (bf16[384,768]{1,0:T(8,128)(2,1)S(1)}, f32[384,128]{1,0:T(8,128)S(1)}, bf16[400,768]{1,0:T(8,128)(2,1)}, bf16[400,768]{1,0:T(8,128)(2,1)}) custom-call(s32[5]{0:T(128)S(1)} %get-tuple-element.19.refs_0_, bf16[384,2048]{1,0:T(8,128)(2,1)S(1)} %copy-done.2, bf16[384,768]{1,0:T(8,128)(2,1)S(1)} %collective-permute-done.4.refs_2_, ...), custom_call_target="tpu_custom_call" | custom-call | flops 4529848320 | bytes 8388608 | tf_op jit(solution)/shard_map/attend/pallas_call | solution.py:490
  91.7 2.1 %collective-permute-start.7 = (bf16[400,768]{1,0:T(8,128)(2,1)}, bf16[400,768]{1,0:T(8,128)(2,1)}, u32[]{:S(2)}, u32[]{:S(2)}) collective-permute-start(bf16[400,768]{1,0:T(8,128)(2,1)} %get-tuple-element.21), channel_id=1, source_target_pairs={{4,8},{8,12},{5,9},{9,13},{6,10},{10,14},{7,11},{11,15},{20,24},{2... | collective-permute-start | bytes 1843208 | tf_op jit(solution)/shard_map/ppermute | solution.py:510
  93.8 2.1 %collective-permute-start.8 = (bf16[400,768]{1,0:T(8,128)(2,1)}, bf16[400,768]{1,0:T(8,128)(2,1)}, u32[]{:S(2)}, u32[]{:S(2)}) collective-permute-start(bf16[400,768]{1,0:T(8,128)(2,1)} %get-tuple-element.22), channel_id=1, source_target_pairs={{4,12},{5,13},{6,14},{7,15},{20,28},{21,29},{22,30},{23,31}} | collective-permute-start | bytes 1843208 | tf_op jit(solution)/shard_map/ppermute | solution.py:511
  95.9 5.9 %near.1.refs_5_ = bf16[384,2048]{1,0:T(8,128)(2,1)} custom-call(s32[5]{0:T(128)S(1)} %get-tuple-element.19.refs_0_, bf16[384,2048]{1,0:T(8,128)(2,1)S(1)} %copy-done.2, bf16[384,2048]{1,0:T(8,128)(2,1)S(1)} %copy-done, bf16[384,2048]{1,0:T(8,128)(2,1)S(1)} %copy-done.1, bf16[384,1024]{1,0:T(8,128)(2,1)S(1)} %collective-permute-done.11.refs_4_.refs_5_, ...), custom_call_target="tpu_custom_call" | custom-call | flops 1811939328 | bytes 4194304 | tf_op jit(solution)/shard_map/near/pallas_call | solution.py:517
  101.8 10.6 %collective-permute-done.9.refs_3_ = bf16[400,768]{1,0:T(8,128)(2,1)S(1)} collective-permute-done((bf16[400,768]{1,0:T(8,128)(2,1)S(1)}, bf16[400,768]{1,0:T(8,128)(2,1)S(1)}, u32[]{:S(2)}, u32[]{:S(2)}) %collective-permute-start.9) | collective-permute-done | bytes 614432 | tf_op jit(solution)/shard_map/ppermute | solution.py:510
  112.4 13.2 %collective-permute-done.10.refs_4_ = bf16[400,768]{1,0:T(8,128)(2,1)S(1)} collective-permute-done((bf16[400,768]{1,0:T(8,128)(2,1)S(1)}, bf16[400,768]{1,0:T(8,128)(2,1)S(1)}, u32[]{:S(2)}, u32[]{:S(2)}) %collective-permute-start.10) | collective-permute-done | bytes 614432 | tf_op jit(solution)/shard_map/ppermute | solution.py:511
  126.4 4.6 %merge.2.refs_5_ = bf16[384,2048]{1,0:T(8,128)(2,1)} custom-call(s32[5]{0:T(128)} %copy-done.9, bf16[384,768]{1,0:T(8,128)(2,1)} %copy-done.4, f32[384,128]{1,0:T(8,128)} %copy-done.7, bf16[400,768]{1,0:T(8,128)(2,1)} %copy-done.13, bf16[400,768]{1,0:T(8,128)(2,1)} %copy-done.14, bf16[384,2048]{1,0:T(8,128)(2,1)} %near.1.refs_5_), custom_call_target="tpu_custom_call", output_to_operand_aliasing={{}: (5, {})} | custom-call | flops 4718592 | bytes 4194304 | tf_op jit(solution)/shard_map/merge/pallas_call | solution.py:534
  131.0 7.8 %collective-permute-done.7.refs_3_ = bf16[400,768]{1,0:T(8,128)(2,1)} collective-permute-done((bf16[400,768]{1,0:T(8,128)(2,1)}, bf16[400,768]{1,0:T(8,128)(2,1)}, u32[]{:S(2)}, u32[]{:S(2)}) %collective-permute-start.7) | collective-permute-done | bytes 614432 | tf_op jit(solution)/shard_map/ppermute | solution.py:510
  138.8 10.2 %collective-permute-done.8.refs_4_ = bf16[400,768]{1,0:T(8,128)(2,1)} collective-permute-done((bf16[400,768]{1,0:T(8,128)(2,1)}, bf16[400,768]{1,0:T(8,128)(2,1)}, u32[]{:S(2)}, u32[]{:S(2)}) %collective-permute-start.8) | collective-permute-done | bytes 614432 | tf_op jit(solution)/shard_map/ppermute | solution.py:511
  149.1 4.6 %merge.3 = bf16[384,2048]{1,0:T(8,128)(2,1)} custom-call(s32[5]{0:T(128)} %copy-done.9, bf16[384,768]{1,0:T(8,128)(2,1)} %copy-done.5, f32[384,128]{1,0:T(8,128)} %copy-done.8, bf16[400,768]{1,0:T(8,128)(2,1)} %collective-permute-done.7.refs_3_, bf16[400,768]{1,0:T(8,128)(2,1)} %collective-permute-done.8.refs_4_, ...), custom_call_target="tpu_custom_call", output_to_operand_aliasing={{}: (5, {})} | custom-call | flops 4718592 | bytes 4194304 | tf_op jit(solution)/shard_map/merge/pallas_call | solution.py:534
  (57 shorter events, 14.3 us)
Async XLA Ops:
  0.6 12.0 %copy-start = (bf16[384,2048]{1,0:T(8,128)(2,1)S(1)}, bf16[384,2048]{1,0:T(8,128)(2,1)}, u32[]{:S(2)}) copy-start(bf16[384,2048]{1,0:T(8,128)(2,1)} %refs_2_.1) | copy-start | bytes 4718596
  0.6 12.0 %copy-start.1 = (bf16[384,2048]{1,0:T(8,128)(2,1)S(1)}, bf16[384,2048]{1,0:T(8,128)(2,1)}, u32[]{:S(2)}) copy-start(bf16[384,2048]{1,0:T(8,128)(2,1)} %refs_3_.1) | copy-start | bytes 4718596
  3.1 23.0 %collective-permute-start.1 = (bf16[384,768]{1,0:T(8,128)(2,1)}, bf16[384,768]{1,0:T(8,128)(2,1)}, u32[]{:S(2)}, u32[]{:S(2)}) collective-permute-start(bf16[384,768]{1,0:T(8,128)(2,1)} %get-tuple-element.31), channel_id=1, source_target_pairs={{8,4},{12,8},{9,5},{13,9},{10,6},{14,10},{11,7},{15,11},{24,20},{2... | collective-permute-start | bytes 1769480 | tf_op jit(solution)/shard_map/ppermute | solution.py:478
  4.4 41.2 %collective-permute-start.2 = (bf16[384,768]{1,0:T(8,128)(2,1)}, bf16[384,768]{1,0:T(8,128)(2,1)}, u32[]{:S(2)}, u32[]{:S(2)}) collective-permute-start(bf16[384,768]{1,0:T(8,128)(2,1)} %get-tuple-element.31), channel_id=1, source_target_pairs={{12,4},{13,5},{14,6},{15,7},{28,20},{29,21},{30,22},{31,23}} | collective-permute-start | bytes 1769480 | tf_op jit(solution)/shard_map/ppermute | solution.py:479
  7.9 17.0 %collective-permute-start = (bf16[128,2048]{1,0:T(8,128)(2,1)}, bf16[128,2048]{1,0:T(8,128)(2,1)}, u32[]{:S(2)}, u32[]{:S(2)}) collective-permute-start(bf16[128,2048]{1,0:T(8,128)(2,1)} %fusion.1), channel_id=1, source_target_pairs={{0,4},{4,8},{8,12},{1,5},{5,9},{9,13},{2,6},{6,10},{10,14},{3,7},{... | collective-permute-start | bytes 1572872 | tf_op jit(solution)/shard_map/ppermute | solution.py:17
  13.9 3.9 %copy-start.12 = (f32[128,2048]{1,0:T(8,128)S(1)}, f32[128,2048]{1,0:T(8,128)}, u32[]{:S(2)}) copy-start(f32[128,2048]{1,0:T(8,128)} %param.12) | copy-start | bytes 3145732
  13.9 36.2 %collective-permute-start.3 = (bf16[384,1536]{1,0:T(8,128)(2,1)}, bf16[384,1536]{1,0:T(8,128)(2,1)}, u32[]{:S(2)}, u32[]{:S(2)}) collective-permute-start(bf16[384,1536]{1,0:T(8,128)(2,1)} %pad_maximum_fusion), channel_id=1, source_target_pairs={{0,4},{1,5},{2,6},{3,7},{16,20},{17,21},{18,22},{19,23}} | collective-permute-start | bytes 3538952 | tf_op jit(solution)/shard_map/ppermute | solution.py:481
  16.4 59.0 %collective-permute-start.6 = (bf16[384,1536]{1,0:T(8,128)(2,1)}, bf16[384,1536]{1,0:T(8,128)(2,1)}, u32[]{:S(2)}, u32[]{:S(2)}) collective-permute-start(bf16[384,1536]{1,0:T(8,128)(2,1)} %pad_maximum_fusion.1), channel_id=1, source_target_pairs={{0,4},{1,5},{2,6},{3,7},{16,20},{17,21},{18,22},{19,23}} | collective-permute-start | bytes 3538952 | tf_op jit(solution)/shard_map/ppermute | solution.py:481
  19.6 7.8 %copy-start.3 = (f32[128,2048]{1,0:T(8,128)S(1)}, f32[128,2048]{1,0:T(8,128)}, u32[]{:S(2)}) copy-start(f32[128,2048]{1,0:T(8,128)} %fusion.refs_3_) | copy-start | bytes 3145732
  19.6 7.8 %copy-start.10 = (bf16[2,256,256]{2,1,0:T(8,128)(2,1)S(1)}, bf16[2,256,256]{2,1,0:T(8,128)(2,1)}, u32[]{:S(2)}) copy-start(bf16[2,256,256]{2,1,0:T(8,128)(2,1)} %constant.14.clone.refs_4_) | copy-start | bytes 786436
  19.6 7.8 %copy-start.11 = (bf16[2,128,256]{2,1,0:T(8,128)(2,1)S(1)}, bf16[2,128,256]{2,1,0:T(8,128)(2,1)}, u32[]{:S(2)}) copy-start(bf16[2,128,256]{2,1,0:T(8,128)(2,1)} %constant.15.clone.refs_5_) | copy-start | bytes 393220
  19.7 76.2 %copy-start.9 = (s32[5]{0:T(128)}, s32[5]{0:T(128)S(1)}, u32[]{:S(2)}) copy-start(s32[5]{0:T(128)S(1)} %get-tuple-element.19.refs_0_) | copy-start | bytes 64
  24.9 43.9 %collective-permute-start.4 = (bf16[384,768]{1,0:T(8,128)(2,1)}, bf16[384,768]{1,0:T(8,128)(2,1)S(1)}, u32[]{:S(2)}, u32[]{:S(2)}) collective-permute-start(bf16[384,768]{1,0:T(8,128)(2,1)} %get-tuple-element.30), channel_id=1, source_target_pairs={{8,4},{12,8},{9,5},{13,9},{10,6},{14,10},{11,7},{15,11},{24,20},{2... | collective-permute-start | bytes 1769480 | tf_op jit(solution)/shard_map/ppermute | solution.py:478
  26.2 43.9 %collective-permute-start.5 = (bf16[384,768]{1,0:T(8,128)(2,1)}, bf16[384,768]{1,0:T(8,128)(2,1)S(1)}, u32[]{:S(2)}, u32[]{:S(2)}) collective-permute-start(bf16[384,768]{1,0:T(8,128)(2,1)} %get-tuple-element.30), channel_id=1, source_target_pairs={{12,4},{13,5},{14,6},{15,7},{28,20},{29,21},{30,22},{31,23}} | collective-permute-start | bytes 1769480 | tf_op jit(solution)/shard_map/ppermute | solution.py:479
  29.8 21.6 %copy-start.2 = (bf16[384,2048]{1,0:T(8,128)(2,1)S(1)}, bf16[384,2048]{1,0:T(8,128)(2,1)}, u32[]{:S(2)}) copy-start(bf16[384,2048]{1,0:T(8,128)(2,1)} %refs_1_.5) | copy-start | bytes 4718596
  45.6 48.2 %collective-permute-start.11 = (bf16[384,1024]{1,0:T(8,128)(2,1)S(1)}, bf16[384,1024]{1,0:T(8,128)(2,1)S(1)}, u32[]{:S(2)}, u32[]{:S(2)}) collective-permute-start(bf16[384,1024]{1,0:T(8,128)(2,1)S(1)} %pad_maximum_fusion.2), channel_id=1, source_target_pairs={{0,4},{4,8},{8,12},{1,5},{5,9},{9,13},{2,6},{6,10},{10,14},{3,7},{... | collective-permute-start | bytes 2359304 | tf_op jit(solution)/shard_map/ppermute | solution.py:483
  50.1 45.8 %collective-permute-start.12 = (bf16[384,1024]{1,0:T(8,128)(2,1)S(1)}, bf16[384,1024]{1,0:T(8,128)(2,1)S(1)}, u32[]{:S(2)}, u32[]{:S(2)}) collective-permute-start(bf16[384,1024]{1,0:T(8,128)(2,1)S(1)} %pad_maximum_fusion.2), channel_id=1, source_target_pairs={{0,8},{4,12},{1,9},{5,13},{2,10},{6,14},{3,11},{7,15},{16,24},{20,... | collective-permute-start | bytes 2359304 | tf_op jit(solution)/shard_map/ppermute | solution.py:484
  68.8 43.6 %collective-permute-start.9 = (bf16[400,768]{1,0:T(8,128)(2,1)S(1)}, bf16[400,768]{1,0:T(8,128)(2,1)S(1)}, u32[]{:S(2)}, u32[]{:S(2)}) collective-permute-start(bf16[400,768]{1,0:T(8,128)(2,1)S(1)} %get-tuple-element.24), channel_id=1, source_target_pairs={{4,8},{8,12},{5,9},{9,13},{6,10},{10,14},{7,11},{11,15},{20,24},{2... | collective-permute-start | bytes 1843208 | tf_op jit(solution)/shard_map/ppermute | solution.py:510
  70.1 55.5 %collective-permute-start.10 = (bf16[400,768]{1,0:T(8,128)(2,1)S(1)}, bf16[400,768]{1,0:T(8,128)(2,1)S(1)}, u32[]{:S(2)}, u32[]{:S(2)}) collective-permute-start(bf16[400,768]{1,0:T(8,128)(2,1)S(1)} %get-tuple-element.25), channel_id=1, source_target_pairs={{4,12},{5,13},{6,14},{7,15},{20,28},{21,29},{22,30},{23,31}} | collective-permute-start | bytes 1843208 | tf_op jit(solution)/shard_map/ppermute | solution.py:511
  91.7 10.1 %copy-start.5 = (bf16[384,768]{1,0:T(8,128)(2,1)}, bf16[384,768]{1,0:T(8,128)(2,1)S(1)}, u32[]{:S(2)}) copy-start(bf16[384,768]{1,0:T(8,128)(2,1)S(1)} %get-tuple-element.18.refs_1_) | copy-start | bytes 1769476
  91.7 10.1 %copy-start.8 = (f32[384,128]{1,0:T(8,128)}, f32[384,128]{1,0:T(8,128)S(1)}, u32[]{:S(2)}) copy-start(f32[384,128]{1,0:T(8,128)S(1)} %get-tuple-element.20.refs_2_) | copy-start | bytes 589828
  91.7 47.1 %collective-permute-start.7 = (bf16[400,768]{1,0:T(8,128)(2,1)}, bf16[400,768]{1,0:T(8,128)(2,1)}, u32[]{:S(2)}, u32[]{:S(2)}) collective-permute-start(bf16[400,768]{1,0:T(8,128)(2,1)} %get-tuple-element.21), channel_id=1, source_target_pairs={{4,8},{8,12},{5,9},{9,13},{6,10},{10,14},{7,11},{11,15},{20,24},{2... | collective-permute-start | bytes 1843208 | tf_op jit(solution)/shard_map/ppermute | solution.py:510
  93.8 55.3 %collective-permute-start.8 = (bf16[400,768]{1,0:T(8,128)(2,1)}, bf16[400,768]{1,0:T(8,128)(2,1)}, u32[]{:S(2)}, u32[]{:S(2)}) collective-permute-start(bf16[400,768]{1,0:T(8,128)(2,1)} %get-tuple-element.22), channel_id=1, source_target_pairs={{4,12},{5,13},{6,14},{7,15},{20,28},{21,29},{22,30},{23,31}} | collective-permute-start | bytes 1843208 | tf_op jit(solution)/shard_map/ppermute | solution.py:511
  112.4 13.2 %copy-start.13 = (bf16[400,768]{1,0:T(8,128)(2,1)}, bf16[400,768]{1,0:T(8,128)(2,1)S(1)}, u32[]{:S(2)}) copy-start(bf16[400,768]{1,0:T(8,128)(2,1)S(1)} %collective-permute-done.9.refs_3_) | copy-start | bytes 1843204
  (8 other events, 16.1 us)

commit v4 on v3

--- a/solution.py
+++ b/solution.py
@@ -276,25 +276,26 @@
     return start
 
 
-def attend(query_ref, keys, values, biases, emit):
+def attend(query_ref, keys, values, biases, backs, emit):
     rows = query_ref.shape[0]
     step = 128
     ones = jnp.ones((rows, 128), jnp.bfloat16)
     vals = [jnp.concatenate((v[...], ones), axis=1) for v in values]
     for r in range(0, rows, step):
         q = query_ref[r : r + step, :]
+        cuts = [(0, r + step) if back == 0 else (r, rows) if back == 2 else (0, rows) for back in backs]
         scores = [
-            lax.dot_general(q, k[...], (((1,), (1,)), ((), ())),
-                            preferred_element_type=jnp.float32) + b[r : r + step, :]
-            for k, b in zip(keys, biases)
+            lax.dot_general(q, k[lo:hi, :], (((1,), (1,)), ((), ())),
+                            preferred_element_type=jnp.float32) + b[r : r + step, lo:hi]
+            for k, b, (lo, hi) in zip(keys, biases, cuts)
         ]
         top = jnp.max(scores[0], axis=1, keepdims=True)
         for s in scores[1:]:
             top = jnp.maximum(top, jnp.max(s, axis=1, keepdims=True))
         acc = None
-        for s, v in zip(scores, vals):
+        for s, v, (lo, hi) in zip(scores, vals, cuts):
             w = jnp.exp2((s - top) * SCALE2).astype(jnp.bfloat16)
-            part = jnp.dot(w, v, preferred_element_type=jnp.float32)
+            part = jnp.dot(w, v[lo:hi], preferred_element_type=jnp.float32)
             acc = part if acc is None else acc + part
         total = acc[:, 128:]
         emit(r, acc[:, :128] / total, top * SCALE2 + jnp.log2(total))
@@ -334,12 +335,12 @@
         o_ref[r : r + 128, :] = out.astype(jnp.bfloat16)
 
     pl.when(two)(
-        lambda: attend(q_ref, (k_ref, k1_ref, k2_ref), (v_ref, v1_ref, v2_ref), (b0, b1, b2), emit)
+        lambda: attend(q_ref, (k_ref, k1_ref, k2_ref), (v_ref, v1_ref, v2_ref), (b0, b1, b2), (0, 1, 2), emit)
     )
     pl.when(one & jnp.logical_not(two))(
-        lambda: attend(q_ref, (k_ref, k1_ref), (v_ref, v1_ref), (b0, b1), emit)
-    )
-    pl.when(jnp.logical_not(one))(lambda: attend(q_ref, (k_ref,), (v_ref,), (b0,), emit))
+        lambda: attend(q_ref, (k_ref, k1_ref), (v_ref, v1_ref), (b0, b1), (0, 1), emit)
+    )
+    pl.when(jnp.logical_not(one))(lambda: attend(q_ref, (k_ref,), (v_ref,), (b0,), (0,), emit))
 
 
 def attn_kernel(rows, lens_ref, q_ref, qa_ref, qb_ref, kp_ref, vp_ref, k_ref, v_ref,
@@ -399,16 +400,16 @@
         ref[:rows, :] = jnp.zeros((rows, 128), jnp.bfloat16)
         ref[rows:, :] = jnp.where(stat_iota < rows // step, NEG, 0.0).astype(jnp.bfloat16)
 
-    pl.when(own_prev)(lambda: attend(q_ref, (kp_ref, k_ref), (vp_ref, v_ref), (b01, b00), emit_own))
-    pl.when(jnp.logical_not(own_prev))(lambda: attend(q_ref, (k_ref,), (v_ref,), (b00,), emit_own))
+    pl.when(own_prev)(lambda: attend(q_ref, (kp_ref, k_ref), (vp_ref, v_ref), (b01, b00), (1, 0), emit_own))
+    pl.when(jnp.logical_not(own_prev))(lambda: attend(q_ref, (k_ref,), (v_ref,), (b00,), (0,), emit_own))
     pl.when(a_prev)(
-        lambda: attend(qa_ref, (kp_ref, k_ref), (vp_ref, v_ref), (b11, b10), emit_to(oa_ref))
+        lambda: attend(qa_ref, (kp_ref, k_ref), (vp_ref, v_ref), (b11, b10), (2, 1), emit_to(oa_ref))
     )
     pl.when(a_here & jnp.logical_not(a_prev))(
-        lambda: attend(qa_ref, (k_ref,), (v_ref,), (b10,), emit_to(oa_ref))
+        lambda: attend(qa_ref, (k_ref,), (v_ref,), (b10,), (1,), emit_to(oa_ref))
     )
     pl.when(jnp.logical_not(a_here))(lambda: empty(oa_ref))
-    pl.when(b_here)(lambda: attend(qb_ref, (k_ref,), (v_ref,), (b02,), emit_to(ob_ref)))
+    pl.when(b_here)(lambda: attend(qb_ref, (k_ref,), (v_ref,), (b02,), (2,), emit_to(ob_ref)))
     pl.when(jnp.logical_not(b_here))(lambda: empty(ob_ref))
 
 
@@ -481,8 +482,8 @@
         sent.append((qa, qb, lax.ppermute(kv, "seq", [(0, 1)])))
     kv = pair(2 * width, cols)
     kv1 = lax.ppermute(kv, "seq", [(0, 1), (1, 2), (2, 3)])
-    kv2 = lax.ppermute(kv, "seq", [(0, 2), (1, 3)])
-    scalars, hyena_out = lax.optimization_barrier((scalars, hyena_out))
+    kv2 = lax.ppermute(kv1, "seq", [(1, 2), (2, 3)])
+    scalars, hyena_out, kv1, kv2 = lax.optimization_barrier((scalars, hyena_out, kv1, kv2))
     outs = []
     for c in range(2):
         qa, qb, kvp = sent[c]

time: 156 us -> 158 us (1.013)
  waiting for transfers between devices: 52.2 us -> 45 us
  starting transfers between devices: 22.9 us -> 28.6 us
  local copies, waits for them, and re-layouts: 8.21 us -> 12 us
  Pallas kernels: 62.9 us -> 64.9 us
  other arithmetic: 6.64 us -> 4.94 us
    ppermute x1, waiting for transfers between devices: 0.01 us -> 20.9 us  [attention_fast(): kv1 = lax.ppermute(kv, 'seq', [(0, 1), (1, 2), (2, 3)])]
    ppermute x2, waiting for transfers between devices: 23.4 us -> 3.99 us  [attention_fast(): rb = lax.ppermute(ob, 'seq', [(1, 3)])]
    ppermute x1, waiting for transfers between devices: 0.01 us -> 9.91 us  [attention_fast(): kv2 = lax.ppermute(kv1, 'seq', [(1, 2), (2, 3)])]
    ppermute x2, waiting for transfers between devices: 18.4 us -> 10.1 us  [attention_fast(): ra = lax.ppermute(oa, 'seq', [(1, 2), (2, 3)])]
    ppermute x2, waiting for transfers between devices: 6.44 us -> 0.01 us  [attention_fast(): sent.append((qa, qb, lax.ppermute(kv, 'seq', [(0, 1)])))]
    unnamed x36 -> x42, local copies, waits for them, and re-layouts: 4.76 us -> 9.47 us
    pallas_call x2, Pallas kernels: 32 us -> 36.2 us  [attention_fast(): pl.pallas_call(lambda *refs: attn_kernel(rows, *refs), grid=(heads,), out...]
    ppermute x1, waiting for transfers between devices: 3.97 us -> 0.01 us  [passed_along(): return lax.ppermute(value, axis, pairs)]
  transfers between devices with their start and end apart: 13 -> 13, of which waited for: 7 -> 4; matrix products, arithmetic and copies ran while one was open for 5% -> 3% of each run, Pallas kernels for 38% -> 39%
where the time goes in v4:
time: 158 us; the launch traced here: 156 us
  Pallas kernels  64.9 us (41%)
  waiting for transfers between devices  45 us (28%)
  starting transfers between devices  28.6 us (18%)
  local copies, waits for them, and re-layouts  12 us (8%)
  other arithmetic  4.94 us (3%)
    pallas_call x2, Pallas kernels, attention_fast(): pl.pallas_call(lambda *refs: attn_kernel(rows, *refs), grid=(heads,), out...  36.2 us
    ppermute x1, waiting for transfers between devices, attention_fast(): kv1 = lax.ppermute(kv, 'seq', [(0, 1), (1, 2), (2, 3)])  20.9 us
    pallas_call x1, Pallas kernels, hyena_fast(): pl.pallas_call(lambda *refs: hyena_kernel(row_count, taps, *refs), grid=(...  13.1 us
    ppermute x2, waiting for transfers between devices, attention_fast(): ra = lax.ppermute(oa, 'seq', [(1, 2), (2, 3)])  10.1 us
    ppermute x1, waiting for transfers between devices, attention_fast(): kv2 = lax.ppermute(kv1, 'seq', [(1, 2), (2, 3)])  9.91 us
    unnamed x42, local copies, waits for them, and re-layouts  9.47 us
    pallas_call x2, Pallas kernels, attention_fast(): pl.pallas_call(lambda *refs: merge_kernel(rows, *refs), grid=(heads,), ou...  9.26 us
    pallas_call x1, Pallas kernels, attention_fast(): pl.pallas_call(lambda *refs: near_kernel(rows, *refs[:8], None, *refs[8:]...  6.26 us
  transfers between devices with their start and end apart: 13, of which 4 were waited for; matrix products, arithmetic and copies ran while one was open for 3% of the time, Pallas kernels for 39%

profile of v4, /device:TPU:10, one launch (start us, length us, event | category | flops | bytes accessed | tf_op | source)
XLA Modules:
  0.0 156.4 jit_solution(2576156858518054238)
XLA Ops:
  0.6 2.3 %fusion.4 = (bf16[384,768]{1,0:T(8,128)(2,1)}, bf16[384,768]{1,0:T(8,128)(2,1)}) fusion(bf16[384,2048]{1,0:T(8,128)(2,1)} %refs_1_.5), kind=kLoop, calls=%fused_computation.13 | loop fusion | bytes 2359296 | tf_op jit(solution)/shard_map/slice | solution.py:478
  3.0 1.3 collective-permute-start.3
  4.2 1.3 collective-permute-start.4
  5.6 1.5 fusion.1
  7.1 4.9 %collective-permute-start = (bf16[128,2048]{1,0:T(8,128)(2,1)S(1)}, bf16[128,2048]{1,0:T(8,128)(2,1)S(1)}, u32[]{:S(2)}, u32[]{:S(2)}) collective-permute-start(bf16[128,2048]{1,0:T(8,128)(2,1)S(1)} %fusion.1), channel_id=1, source_target_pairs={{0,4},{4,8},{8,12},{1,5},{5,9},{9,13},{2,6},{6,10},{10,14},{3,7},{... | collective-permute-start | bytes 1572872 | tf_op jit(solution)/shard_map/ppermute | solution.py:17
  12.1 5.0 %collective-permute-start.1 = (bf16[384,1024]{1,0:T(8,128)(2,1)S(1)}, bf16[384,1024]{1,0:T(8,128)(2,1)S(1)}, u32[]{:S(2)}, u32[]{:S(2)}) collective-permute-start(bf16[384,1024]{1,0:T(8,128)(2,1)S(1)} %pad_maximum_fusion.2), channel_id=1, source_target_pairs={{0,4},{4,8},{8,12},{1,5},{5,9},{9,13},{2,6},{6,10},{10,14},{3,7},{... | collective-permute-start | bytes 2359304 | tf_op jit(solution)/shard_map/ppermute | solution.py:484
  18.4 1.4 collective-permute-start.5
  19.8 20.9 %collective-permute-done.1.refs_4_.refs_5_ = bf16[384,1024]{1,0:T(8,128)(2,1)S(1)} collective-permute-done((bf16[384,1024]{1,0:T(8,128)(2,1)S(1)}, bf16[384,1024]{1,0:T(8,128)(2,1)S(1)}, u32[]{:S(2)}, u32[]{:S(2)}) %collective-permute-start.1) | collective-permute-done | bytes 786464 | tf_op jit(solution)/shard_map/ppermute | solution.py:484
  40.8 3.9 %collective-permute-start.2 = (bf16[384,1024]{1,0:T(8,128)(2,1)S(1)}, bf16[384,1024]{1,0:T(8,128)(2,1)S(1)}, u32[]{:S(2)}, u32[]{:S(2)}) collective-permute-start(bf16[384,1024]{1,0:T(8,128)(2,1)S(1)} %collective-permute-done.1.refs_4_.refs_5_), channel_id=1, source_target_pairs={{4,8},{8,12},{5,9},{9,13},{6,10},{10,14},{7,11},{11,15},{20,24},{2... | collective-permute-start | bytes 2359304 | tf_op jit(solution)/shard_map/ppermute | solution.py:485
  49.0 1.3 collective-permute-start.6
  50.3 9.9 %collective-permute-done.2.refs_6_.refs_7_ = bf16[384,1024]{1,0:T(8,128)(2,1)S(1)} collective-permute-done((bf16[384,1024]{1,0:T(8,128)(2,1)S(1)}, bf16[384,1024]{1,0:T(8,128)(2,1)S(1)}, u32[]{:S(2)}, u32[]{:S(2)}) %collective-permute-start.2) | collective-permute-done | bytes 786464 | tf_op jit(solution)/shard_map/ppermute | solution.py:485
  62.8 2.3 %copy-done.7 = bf16[384,3,2048]{2,0,1:T(8,128)(2,1)S(1)} copy-done((bf16[384,3,2048]{2,0,1:T(8,128)(2,1)S(1)}, bf16[384,3,2048]{2,0,1:T(8,128)(2,1)}, u32[]{:S(2)}) %copy-start.7) | copy-done | bytes 4718616
  67.0 13.1 %hyena.1 = bf16[384,2048]{1,0:T(8,128)(2,1)} custom-call(s32[5]{0:T(128)S(1)} %get-tuple-element.36.refs_0_, bf16[3,384,2048]{2,1,0:T(8,128)(2,1)S(1)} %bitcast.7, bf16[128,2048]{1,0:T(8,128)(2,1)S(1)} %copy-done.12, f32[128,2048]{1,0:T(8,128)S(1)} %copy-done.4, bf16[2,256,256]{2,1,0:T(8,128)(2,1)S(1)} %copy-done.13, bf16[2,128,256]{2,1,0:T(8,128)(2,1)S(1)} %copy-done.14), custom_call_target="tpu_custom_call" | custom-call | flops 3623878656 | bytes 8388608 | tf_op jit(solution)/shard_map/hyena/pallas_call | solution.py:245
  80.2 17.8 %attend.2 = (bf16[384,768]{1,0:T(8,128)(2,1)S(1)}, f32[384,128]{1,0:T(8,128)S(1)}, bf16[400,768]{1,0:T(8,128)(2,1)S(1)}, bf16[400,768]{1,0:T(8,128)(2,1)S(1)}) custom-call(s32[5]{0:T(128)S(1)} %get-tuple-element.21.refs_0_, bf16[384,2048]{1,0:T(8,128)(2,1)S(1)} %copy-done.3, bf16[384,768]{1,0:T(8,128)(2,1)} %collective-permute-done.3.refs_2_, ...), custom_call_target="tpu_custom_call" | custom-call | flops 4529848320 | bytes 8388608 | tf_op jit(solution)/shard_map/attend/pallas_call | solution.py:491
  99.5 1.3 collective-permute-start.11
  100.9 1.5 collective-permute-start.12
  102.4 18.4 %attend.3 = (bf16[384,768]{1,0:T(8,128)(2,1)S(1)}, f32[384,128]{1,0:T(8,128)S(1)}, bf16[400,768]{1,0:T(8,128)(2,1)}, bf16[400,768]{1,0:T(8,128)(2,1)}) custom-call(s32[5]{0:T(128)S(1)} %get-tuple-element.21.refs_0_, bf16[384,2048]{1,0:T(8,128)(2,1)S(1)} %copy-done.3, bf16[384,768]{1,0:T(8,128)(2,1)S(1)} %collective-permute-done.6.refs_2_, ...), custom_call_target="tpu_custom_call" | custom-call | flops 4529848320 | bytes 8388608 | tf_op jit(solution)/shard_map/attend/pallas_call | solution.py:491
  120.8 2.1 %collective-permute-start.10 = (bf16[400,768]{1,0:T(8,128)(2,1)}, bf16[400,768]{1,0:T(8,128)(2,1)}, u32[]{:S(2)}, u32[]{:S(2)}) collective-permute-start(bf16[400,768]{1,0:T(8,128)(2,1)} %get-tuple-element.24), channel_id=1, source_target_pairs={{4,12},{5,13},{6,14},{7,15},{20,28},{21,29},{22,30},{23,31}} | collective-permute-start | bytes 1843208 | tf_op jit(solution)/shard_map/ppermute | solution.py:512
  122.9 2.1 %collective-permute-start.9 = (bf16[400,768]{1,0:T(8,128)(2,1)}, bf16[400,768]{1,0:T(8,128)(2,1)}, u32[]{:S(2)}, u32[]{:S(2)}) collective-permute-start(bf16[400,768]{1,0:T(8,128)(2,1)} %get-tuple-element.23), channel_id=1, source_target_pairs={{4,8},{8,12},{5,9},{9,13},{6,10},{10,14},{7,11},{11,15},{20,24},{2... | collective-permute-start | bytes 1843208 | tf_op jit(solution)/shard_map/ppermute | solution.py:511
  125.1 6.3 %near.1.refs_5_ = bf16[384,2048]{1,0:T(8,128)(2,1)} custom-call(s32[5]{0:T(128)S(1)} %get-tuple-element.21.refs_0_, bf16[384,2048]{1,0:T(8,128)(2,1)S(1)} %copy-done.3, bf16[384,2048]{1,0:T(8,128)(2,1)S(1)} %copy-done, bf16[384,2048]{1,0:T(8,128)(2,1)S(1)} %copy-done.2, bf16[384,1024]{1,0:T(8,128)(2,1)S(1)} %collective-permute-done.1.refs_4_.refs_5_, ...), custom_call_target="tpu_custom_call" | custom-call | flops 1811939328 | bytes 4194304 | tf_op jit(solution)/shard_map/near/pallas_call | solution.py:518
  133.0 4.6 %merge.2.refs_5_ = bf16[384,2048]{1,0:T(8,128)(2,1)} custom-call(s32[5]{0:T(128)} %copy-done.10, bf16[384,768]{1,0:T(8,128)(2,1)} %copy-done.5, f32[384,128]{1,0:T(8,128)} %copy-done.8, bf16[400,768]{1,0:T(8,128)(2,1)} %copy-done.16, bf16[400,768]{1,0:T(8,128)(2,1)} %copy-done.17, bf16[384,2048]{1,0:T(8,128)(2,1)} %near.1.refs_5_), custom_call_target="tpu_custom_call", output_to_operand_aliasing={{}: (5, {})} | custom-call | flops 4718592 | bytes 4194304 | tf_op jit(solution)/shard_map/merge/pallas_call | solution.py:535
  137.6 4.0 %collective-permute-done.10.refs_4_ = bf16[400,768]{1,0:T(8,128)(2,1)} collective-permute-done((bf16[400,768]{1,0:T(8,128)(2,1)}, bf16[400,768]{1,0:T(8,128)(2,1)}, u32[]{:S(2)}, u32[]{:S(2)}) %collective-permute-start.10) | collective-permute-done | bytes 614432 | tf_op jit(solution)/shard_map/ppermute | solution.py:512
  141.6 10.1 %collective-permute-done.9.refs_3_ = bf16[400,768]{1,0:T(8,128)(2,1)} collective-permute-done((bf16[400,768]{1,0:T(8,128)(2,1)}, bf16[400,768]{1,0:T(8,128)(2,1)}, u32[]{:S(2)}, u32[]{:S(2)}) %collective-permute-start.9) | collective-permute-done | bytes 614432 | tf_op jit(solution)/shard_map/ppermute | solution.py:511
  151.7 4.6 %merge.3 = bf16[384,2048]{1,0:T(8,128)(2,1)} custom-call(s32[5]{0:T(128)} %copy-done.10, bf16[384,768]{1,0:T(8,128)(2,1)} %copy-done.6, f32[384,128]{1,0:T(8,128)} %copy-done.9, bf16[400,768]{1,0:T(8,128)(2,1)} %collective-permute-done.9.refs_3_, bf16[400,768]{1,0:T(8,128)(2,1)} %collective-permute-done.10.refs_4_, ...), custom_call_target="tpu_custom_call", output_to_operand_aliasing={{}: (5, {})} | custom-call | flops 4718592 | bytes 4194304 | tf_op jit(solution)/shard_map/merge/pallas_call | solution.py:535
  (64 shorter events, 13.4 us)
Async XLA Ops:
  3.0 46.1 %collective-permute-start.3 = (bf16[384,768]{1,0:T(8,128)(2,1)}, bf16[384,768]{1,0:T(8,128)(2,1)}, u32[]{:S(2)}, u32[]{:S(2)}) collective-permute-start(bf16[384,768]{1,0:T(8,128)(2,1)} %get-tuple-element.35), channel_id=1, source_target_pairs={{8,4},{12,8},{9,5},{13,9},{10,6},{14,10},{11,7},{15,11},{24,20},{2... | collective-permute-start | bytes 1769480 | tf_op jit(solution)/shard_map/ppermute | solution.py:479
  4.2 75.9 %collective-permute-start.4 = (bf16[384,768]{1,0:T(8,128)(2,1)}, bf16[384,768]{1,0:T(8,128)(2,1)}, u32[]{:S(2)}, u32[]{:S(2)}) collective-permute-start(bf16[384,768]{1,0:T(8,128)(2,1)} %get-tuple-element.35), channel_id=1, source_target_pairs={{12,4},{13,5},{14,6},{15,7},{28,20},{29,21},{30,22},{31,23}} | collective-permute-start | bytes 1769480 | tf_op jit(solution)/shard_map/ppermute | solution.py:480
  5.5 6.4 %slice-start = ((bf16[384,2048]{1,0:T(8,128)(2,1)}), bf16[384,512]{1,0:T(8,128)(2,1)S(1)}, s32[]{:S(2)}) async-start(bf16[384,2048]{1,0:T(8,128)(2,1)} %refs_2_.1), calls=%async_computation | async-start | bytes 786432 | tf_op jit(solution)/shard_map/slice | solution.py:474
  5.6 6.4 %slice-start.1 = ((bf16[384,2048]{1,0:T(8,128)(2,1)}), bf16[384,512]{1,0:T(8,128)(2,1)S(1)}, s32[]{:S(2)}) async-start(bf16[384,2048]{1,0:T(8,128)(2,1)} %refs_3_.1), calls=%async_computation.1 | async-start | bytes 786432 | tf_op jit(solution)/shard_map/slice | solution.py:474
  5.6 11.5 %copy-start.1 = (bf16[384,2048]{1,0:T(8,128)(2,1)S(1)}, bf16[384,2048]{1,0:T(8,128)(2,1)}, u32[]{:S(2)}) copy-start(bf16[384,2048]{1,0:T(8,128)(2,1)} %refs_3_.1) | copy-start | bytes 4718596
  7.1 10.0 %copy-start = (bf16[384,2048]{1,0:T(8,128)(2,1)S(1)}, bf16[384,2048]{1,0:T(8,128)(2,1)}, u32[]{:S(2)}) copy-start(bf16[384,2048]{1,0:T(8,128)(2,1)} %refs_2_.1) | copy-start | bytes 4718596
  7.1 38.7 %collective-permute-start = (bf16[128,2048]{1,0:T(8,128)(2,1)S(1)}, bf16[128,2048]{1,0:T(8,128)(2,1)S(1)}, u32[]{:S(2)}, u32[]{:S(2)}) collective-permute-start(bf16[128,2048]{1,0:T(8,128)(2,1)S(1)} %fusion.1), channel_id=1, source_target_pairs={{0,4},{4,8},{8,12},{1,5},{5,9},{9,13},{2,6},{6,10},{10,14},{3,7},{... | collective-permute-start | bytes 1572872 | tf_op jit(solution)/shard_map/ppermute | solution.py:17
  12.1 28.7 %collective-permute-start.1 = (bf16[384,1024]{1,0:T(8,128)(2,1)S(1)}, bf16[384,1024]{1,0:T(8,128)(2,1)S(1)}, u32[]{:S(2)}, u32[]{:S(2)}) collective-permute-start(bf16[384,1024]{1,0:T(8,128)(2,1)S(1)} %pad_maximum_fusion.2), channel_id=1, source_target_pairs={{0,4},{4,8},{8,12},{1,5},{5,9},{9,13},{2,6},{6,10},{10,14},{3,7},{... | collective-permute-start | bytes 2359304 | tf_op jit(solution)/shard_map/ppermute | solution.py:484
  18.4 29.5 %copy-start.15 = (f32[128,2048]{1,0:T(8,128)S(1)}, f32[128,2048]{1,0:T(8,128)}, u32[]{:S(2)}) copy-start(f32[128,2048]{1,0:T(8,128)} %param.12) | copy-start | bytes 3145732
  18.4 61.8 %collective-permute-start.5 = (bf16[384,1536]{1,0:T(8,128)(2,1)}, bf16[384,1536]{1,0:T(8,128)(2,1)}, u32[]{:S(2)}, u32[]{:S(2)}) collective-permute-start(bf16[384,1536]{1,0:T(8,128)(2,1)} %pad_maximum_fusion), channel_id=1, source_target_pairs={{0,4},{1,5},{2,6},{3,7},{16,20},{17,21},{18,22},{19,23}} | collective-permute-start | bytes 3538952 | tf_op jit(solution)/shard_map/ppermute | solution.py:482
  40.8 19.4 %collective-permute-start.2 = (bf16[384,1024]{1,0:T(8,128)(2,1)S(1)}, bf16[384,1024]{1,0:T(8,128)(2,1)S(1)}, u32[]{:S(2)}, u32[]{:S(2)}) collective-permute-start(bf16[384,1024]{1,0:T(8,128)(2,1)S(1)} %collective-permute-done.1.refs_4_.refs_5_), channel_id=1, source_target_pairs={{4,8},{8,12},{5,9},{9,13},{6,10},{10,14},{7,11},{11,15},{20,24},{2... | collective-permute-start | bytes 2359304 | tf_op jit(solution)/shard_map/ppermute | solution.py:485
  45.8 15.7 %copy-start.13 = (bf16[2,256,256]{2,1,0:T(8,128)(2,1)S(1)}, bf16[2,256,256]{2,1,0:T(8,128)(2,1)}, u32[]{:S(2)}) copy-start(bf16[2,256,256]{2,1,0:T(8,128)(2,1)} %constant.14.clone.refs_4_) | copy-start | bytes 786436
  46.6 55.8 %collective-permute-start.8 = (bf16[384,1536]{1,0:T(8,128)(2,1)}, bf16[384,1536]{1,0:T(8,128)(2,1)}, u32[]{:S(2)}, u32[]{:S(2)}) collective-permute-start(bf16[384,1536]{1,0:T(8,128)(2,1)} %pad_maximum_fusion.1), channel_id=1, source_target_pairs={{0,4},{1,5},{2,6},{3,7},{16,20},{17,21},{18,22},{19,23}} | collective-permute-start | bytes 3538952 | tf_op jit(solution)/shard_map/ppermute | solution.py:482
  49.0 76.0 %copy-start.10 = (s32[5]{0:T(128)}, s32[5]{0:T(128)S(1)}, u32[]{:S(2)}) copy-start(s32[5]{0:T(128)S(1)} %get-tuple-element.21.refs_0_) | copy-start | bytes 64
  49.0 53.4 %collective-permute-start.6 = (bf16[384,768]{1,0:T(8,128)(2,1)}, bf16[384,768]{1,0:T(8,128)(2,1)S(1)}, u32[]{:S(2)}, u32[]{:S(2)}) collective-permute-start(bf16[384,768]{1,0:T(8,128)(2,1)} %get-tuple-element.34), channel_id=1, source_target_pairs={{8,4},{12,8},{9,5},{13,9},{10,6},{14,10},{11,7},{15,11},{24,20},{2... | collective-permute-start | bytes 1769480 | tf_op jit(solution)/shard_map/ppermute | solution.py:479
  60.2 42.2 %collective-permute-start.7 = (bf16[384,768]{1,0:T(8,128)(2,1)}, bf16[384,768]{1,0:T(8,128)(2,1)S(1)}, u32[]{:S(2)}, u32[]{:S(2)}) collective-permute-start(bf16[384,768]{1,0:T(8,128)(2,1)} %get-tuple-element.34), channel_id=1, source_target_pairs={{12,4},{13,5},{14,6},{15,7},{28,20},{29,21},{30,22},{31,23}} | collective-permute-start | bytes 1769480 | tf_op jit(solution)/shard_map/ppermute | solution.py:480
  67.0 13.2 %copy-start.2 = (bf16[384,2048]{1,0:T(8,128)(2,1)S(1)}, bf16[384,2048]{1,0:T(8,128)(2,1)}, u32[]{:S(2)}) copy-start(bf16[384,2048]{1,0:T(8,128)(2,1)} %refs_3_.1) | copy-start | bytes 4718596
  67.0 13.2 %copy-start.3 = (bf16[384,2048]{1,0:T(8,128)(2,1)S(1)}, bf16[384,2048]{1,0:T(8,128)(2,1)}, u32[]{:S(2)}) copy-start(bf16[384,2048]{1,0:T(8,128)(2,1)} %refs_1_.5) | copy-start | bytes 4718596
  99.5 31.8 %collective-permute-start.11 = (bf16[400,768]{1,0:T(8,128)(2,1)S(1)}, bf16[400,768]{1,0:T(8,128)(2,1)S(1)}, u32[]{:S(2)}, u32[]{:S(2)}) collective-permute-start(bf16[400,768]{1,0:T(8,128)(2,1)S(1)} %get-tuple-element.26), channel_id=1, source_target_pairs={{4,8},{8,12},{5,9},{9,13},{6,10},{10,14},{7,11},{11,15},{20,24},{2... | collective-permute-start | bytes 1843208 | tf_op jit(solution)/shard_map/ppermute | solution.py:511
  100.9 30.5 %collective-permute-start.12 = (bf16[400,768]{1,0:T(8,128)(2,1)S(1)}, bf16[400,768]{1,0:T(8,128)(2,1)S(1)}, u32[]{:S(2)}, u32[]{:S(2)}) collective-permute-start(bf16[400,768]{1,0:T(8,128)(2,1)S(1)} %get-tuple-element.27), channel_id=1, source_target_pairs={{4,12},{5,13},{6,14},{7,15},{20,28},{21,29},{22,30},{23,31}} | collective-permute-start | bytes 1843208 | tf_op jit(solution)/shard_map/ppermute | solution.py:512
  120.8 10.5 %copy-start.6 = (bf16[384,768]{1,0:T(8,128)(2,1)}, bf16[384,768]{1,0:T(8,128)(2,1)S(1)}, u32[]{:S(2)}) copy-start(bf16[384,768]{1,0:T(8,128)(2,1)S(1)} %get-tuple-element.20.refs_1_) | copy-start | bytes 1769476
  120.8 10.5 %copy-start.9 = (f32[384,128]{1,0:T(8,128)}, f32[384,128]{1,0:T(8,128)S(1)}, u32[]{:S(2)}) copy-start(f32[384,128]{1,0:T(8,128)S(1)} %get-tuple-element.22.refs_2_) | copy-start | bytes 589828
  120.8 20.8 %collective-permute-start.10 = (bf16[400,768]{1,0:T(8,128)(2,1)}, bf16[400,768]{1,0:T(8,128)(2,1)}, u32[]{:S(2)}, u32[]{:S(2)}) collective-permute-start(bf16[400,768]{1,0:T(8,128)(2,1)} %get-tuple-element.24), channel_id=1, source_target_pairs={{4,12},{5,13},{6,14},{7,15},{20,28},{21,29},{22,30},{23,31}} | collective-permute-start | bytes 1843208 | tf_op jit(solution)/shard_map/ppermute | solution.py:512
  122.9 28.8 %collective-permute-start.9 = (bf16[400,768]{1,0:T(8,128)(2,1)}, bf16[400,768]{1,0:T(8,128)(2,1)}, u32[]{:S(2)}, u32[]{:S(2)}) collective-permute-start(bf16[400,768]{1,0:T(8,128)(2,1)} %get-tuple-element.23), channel_id=1, source_target_pairs={{4,8},{8,12},{5,9},{9,13},{6,10},{10,14},{7,11},{11,15},{20,24},{2... | collective-permute-start | bytes 1843208 | tf_op jit(solution)/shard_map/ppermute | solution.py:511
  (12 other events, 17.8 us)
